TPU v7x, 32 devices: a whole 2x2x4 slice. The times are simulated.
32 devices in a mesh: scen: 8 (over y, x, core), bldg: 4 (over z).
Axes of the slice: x: 2, y: 2, z: 4, core: 2. Of those that a mesh axis runs over, the one named last changes fastest.
Arguments:
- demand: float32 [128, 1024, 96], P('scen', 'bldg'), may hold values from -6 to 6
- tariff: float32 [128, 96], P('scen'), may hold values from 0 to 0.5
- feeder_price: float32 [128, 8, 96], P('scen'), may hold values from 0 to 0.5
- multiplier: float32 [128, 1024, 96], P('scen', 'bldg'), may hold values from -2 to 2
- previous_mean: float32 [128, 1024, 96], P('scen', 'bldg'), may hold values from 0 to 1
- inverse: float32 [1024, 96, 96], P('bldg'), as said below
- power_limit: float32 [1024, 96], P('bldg'), may hold values from 0.5 to 2
- weights: float32 [128], P('scen'), may hold values from 0.1 to 1
- tree_node: int32 [2, 128], P(None, 'scen'), may hold values from 0 to 15, as said below
- building_feeder: int32 [1024], P('bldg'), may hold values from 0 to 7, as said below
- feeder_limit: float32 [8, 96], replicated, may hold values from 25.6 to 128
Outputs:
- plan: float32 [128, 1024, 96], P('scen', 'bldg')
- new_multiplier: float32 [128, 1024, 96], P('scen', 'bldg')
- new_price: float32 [128, 8, 96], P('scen')
Inputs may be any that keep to these rules, and one draw needn't show every extreme that they name: `tree_node`: scenarios that share a third-section node share the second-section node; each third-section node holds 8 scenarios, each second-section node 16 scenarios. `building_feeder`: every feeder has exactly 128 buildings. `inverse`: symmetric with a positive diagonal.
All inputs are finite; a program needn't handle non-finite values.
Results may differ from a plain program's by a relative error of at most 0.0001.
Values sent between devices are 32-bit elements; how exact they have to be, the bound alone decides.
A program may use at most 128 MiB of HBM per device.

v0:
```python
import functools

import jax
import jax.numpy as jnp
from jax import lax
from jax.experimental import pallas as pl
from jax.experimental.pallas import tpu as pltpu
from jax.sharding import PartitionSpec as P

FEED = 128
PROX = 12


BLOCK = 64
LANES = 128


def prox_kernel(
    demand_ref, tariff_ref, price_ref, mult_ref, prev_ref, inv_ref, limit_ref, feeder_ref,
    plan_ref, load_ref, w_ref, fixed_ref, z_ref, u_ref, price_t_ref,
):
    step = pl.program_id(0)
    scen, block, slots = demand_ref.shape

    @pl.when(step == 0)
    def _():
        load_ref[...] = jnp.zeros_like(load_ref)
        price_t_ref[...] = tariff_ref[...][None] + jnp.transpose(price_ref[...], (1, 0, 2))

    prev = jnp.transpose(prev_ref[...], (1, 0, 2))
    rest = 0.5 * prev_ref[...] + demand_ref[...] - mult_ref[...]
    fixed_ref[...] = jnp.transpose(rest, (1, 0, 2))
    ceiling = limit_ref[...][:, None, :]
    z_ref[...] = jnp.clip(prev, 0.0, ceiling)
    u_ref[...] = jnp.zeros_like(u_ref)
    for b in range(block):
        fixed_ref[b] = fixed_ref[b] - price_t_ref[feeder_ref[step * block + b]]
        full = inv_ref[b]
        high = full.astype(jnp.bfloat16)
        w_ref[b, :, :slots] = high
        w_ref[b, :, LANES : LANES + slots] = (full - high.astype(jnp.float32)).astype(jnp.bfloat16)

    def iteration(i, carry):
        for b in range(block):
            z, u = z_ref[b], u_ref[b]
            right = z - u + fixed_ref[b]
            high = right.astype(jnp.bfloat16)
            low = (right - high.astype(jnp.float32)).astype(jnp.bfloat16)
            both = jnp.concatenate([high, low], axis=0)
            out = jnp.dot(both, w_ref[b], preferred_element_type=jnp.float32)
            primal = out[:scen, :slots] + (out[:scen, LANES : LANES + slots] + out[scen:, :slots])
            moved = primal + u
            fresh = jnp.clip(moved, 0.0, limit_ref[b : b + 1, :])
            z_ref[b] = fresh
            u_ref[b] = moved - fresh
        return carry

    lax.fori_loop(0, PROX, iteration, 0)
    for b in range(block):
        load_ref[feeder_ref[step * block + b]] += z_ref[b]
    plan_ref[...] = jnp.transpose(z_ref[...], (1, 0, 2))


def prox(demand, tariff, feeder_price, multiplier, previous_mean, inverse, power_limit, building_feeder):
    scen, count, slots = demand.shape
    feeders = feeder_price.shape[1]
    block = min(BLOCK, count)
    big = pl.BlockSpec((scen, block, slots), lambda i: (0, i, 0))
    whole2 = pl.BlockSpec((scen, slots), lambda i: (0, 0))
    whole3 = pl.BlockSpec((scen, feeders, slots), lambda i: (0, 0, 0))
    return pl.pallas_call(
        prox_kernel,
        grid=(count // block,),
        in_specs=[
            big, whole2, whole3, big, big,
            pl.BlockSpec((block, slots, slots), lambda i: (i, 0, 0)),
            pl.BlockSpec((block, slots), lambda i: (i, 0)),
            pl.BlockSpec(memory_space=pltpu.SMEM),
        ],
        out_specs=[big, pl.BlockSpec((feeders, scen, slots), lambda i: (0, 0, 0))],
        out_shape=[
            jax.ShapeDtypeStruct((scen, count, slots), jnp.float32),
            jax.ShapeDtypeStruct((feeders, scen, slots), jnp.float32),
        ],
        scratch_shapes=[
            pltpu.VMEM((block, slots, 2 * LANES), jnp.bfloat16),
            pltpu.VMEM((block, scen, slots), jnp.float32),
            pltpu.VMEM((block, scen, slots), jnp.float32),
            pltpu.VMEM((block, scen, slots), jnp.float32),
            pltpu.VMEM((feeders, scen, slots), jnp.float32),
        ],
        compiler_params=pltpu.CompilerParams(dimension_semantics=("arbitrary",), vmem_limit_bytes=40 * 2**20),
        name="prox",
    )(demand, tariff, feeder_price, multiplier, previous_mean, inverse, power_limit, building_feeder)


COARSE = 8


def sums_kernel(weighted_ref, plan_ref, out_ref):
    nodes, scen = weighted_ref.shape
    lanes = plan_ref.shape[2]
    length = plan_ref.shape[1] // 4
    tail = nodes * length
    out_ref[pl.ds(tail, out_ref.shape[0] - tail), :] = jnp.zeros((out_ref.shape[0] - tail, lanes), jnp.float32)

    def add_node(level):
        def body(n, carry):
            factor = weighted_ref[n, 0]
            total = factor
            acc = factor * plan_ref[0, level * length : (level + 1) * length, :]
            for s in range(1, scen):
                factor = weighted_ref[n, s]
                total = total + factor
                acc = acc + factor * plan_ref[s, level * length : (level + 1) * length, :]
            out_ref[pl.ds(pl.multiple_of(n * length, 8), length), :] = acc
            out_ref[pl.ds(tail + n, 1), :] = jnp.full((1, lanes), total, jnp.float32)
            return carry

        return body

    for level, (low, high) in enumerate(((0, 1), (1, 1 + COARSE), (1 + COARSE, nodes))):
        lax.fori_loop(low, high, add_node(level), 0)


def node_sums(weighted, plan_t, length, devices):
    nodes = weighted.shape[0]
    unit = 8 * devices
    rows = (nodes * length + nodes + unit - 1) // unit * unit
    return pl.pallas_call(
        sums_kernel,
        in_specs=[pl.BlockSpec(memory_space=pltpu.SMEM), pl.BlockSpec(memory_space=pltpu.VMEM)],
        out_specs=pl.BlockSpec(memory_space=pltpu.VMEM),
        out_shape=jax.ShapeDtypeStruct((rows, plan_t.shape[2]), jnp.float32),
        compiler_params=pltpu.CompilerParams(vmem_limit_bytes=24 * 2**20),
        name="node_sums",
    )(weighted, plan_t)


def exchange_kernel(
    scen_size, bldg_size, sums_ref, load_ref, full_ref, total_ref,
    landed, own, load_landed, all_rows, rs_send, rs_recv, ag_send, ag_recv, load_send, load_recv,
):
    me, column = lax.axis_index("scen"), lax.axis_index("bldg")
    chunk = own.shape[0]
    peers = [(lax.rem(me + k, scen_size), column) for k in range(1, scen_size)]
    beside = [(me, lax.rem(column + k, bldg_size)) for k in range(1, bldg_size)]
    barrier = pltpu.get_barrier_semaphore()
    for peer in peers + beside:
        pl.semaphore_signal(barrier, inc=1, device_id=peer, device_id_type=pl.DeviceIdType.MESH)
    pl.semaphore_wait(barrier, scen_size + bldg_size - 2)

    def rows_of(index):
        return pl.ds(pl.multiple_of(index * chunk, 8), chunk)

    scatter = []
    for k, peer in enumerate(peers):
        copy = pltpu.make_async_remote_copy(
            src_ref=sums_ref.at[rows_of(peer[0])], dst_ref=landed.at[k],
            send_sem=rs_send.at[k], recv_sem=rs_recv.at[k],
            device_id=peer, device_id_type=pl.DeviceIdType.MESH,
        )
        copy.start()
        scatter.append(copy)
    loads = []
    for k, peer in enumerate(beside):
        copy = pltpu.make_async_remote_copy(
            src_ref=load_ref, dst_ref=load_landed.at[k],
            send_sem=load_send.at[k], recv_sem=load_recv.at[k],
            device_id=peer, device_id_type=pl.DeviceIdType.MESH,
        )
        copy.start()
        loads.append(copy)
    for copy in scatter:
        copy.wait_recv()
    acc = sums_ref[rows_of(me), :]
    for k in range(scen_size - 1):
        acc = acc + landed[k]
    own[...] = acc
    all_rows[rows_of(me), :] = acc
    gather = []
    for k, peer in enumerate(peers):
        copy = pltpu.make_async_remote_copy(
            src_ref=own, dst_ref=all_rows.at[rows_of(me)],
            send_sem=ag_send.at[k], recv_sem=ag_recv.at[k],
            device_id=peer, device_id_type=pl.DeviceIdType.MESH,
        )
        copy.start()
        gather.append(copy)
    for copy in loads:
        copy.wait_recv()
    total = load_ref[...]
    for k in range(bldg_size - 1):
        total = total + load_landed[k]
    total_ref[...] = total
    for copy in gather:
        copy.wait_recv()
    full_ref[...] = all_rows[...]
    for copy in scatter + loads + gather:
        copy.wait_send()


def exchange(local, load):
    scen_size, bldg_size = lax.axis_size("scen"), lax.axis_size("bldg")
    rows, lanes = local.shape
    chunk = rows // scen_size
    dma = pltpu.SemaphoreType.DMA
    vmem = pl.BlockSpec(memory_space=pltpu.VMEM)
    return pl.pallas_call(
        functools.partial(exchange_kernel, scen_size, bldg_size),
        in_specs=[vmem, vmem],
        out_specs=[vmem, vmem],
        out_shape=[
            jax.ShapeDtypeStruct((rows, lanes), jnp.float32),
            jax.ShapeDtypeStruct(load.shape, jnp.float32),
        ],
        scratch_shapes=[
            pltpu.VMEM((scen_size - 1, chunk, lanes), jnp.float32),
            pltpu.VMEM((chunk, lanes), jnp.float32),
            pltpu.VMEM((bldg_size - 1,) + load.shape, jnp.float32),
            pltpu.VMEM((rows, lanes), jnp.float32),
            dma((scen_size - 1,)), dma((scen_size - 1,)),
            dma((scen_size - 1,)), dma((scen_size - 1,)),
            dma((bldg_size - 1,)), dma((bldg_size - 1,)),
        ],
        compiler_params=pltpu.CompilerParams(
            collective_id=0, has_side_effects=True, vmem_limit_bytes=24 * 2**20
        ),
        name="exchange",
    )(local, load)


def spread_kernel(nodes, places_ref, full_ref, plan_ref, mult_ref, out_ref, mean_ref):
    scen, slots, _ = plan_ref.shape
    length = slots // 4
    tail = nodes * length

    def divide(n, carry):
        share = full_ref[pl.ds(pl.multiple_of(n * length, 8), length), :]
        mean_ref[n] = share / full_ref[pl.ds(tail + n, 1), :]
        return carry

    lax.fori_loop(0, nodes, divide, 0)
    for s in range(scen):
        for level in range(4):
            part = slice(level * length, (level + 1) * length)
            plan = plan_ref[s, part, :]
            mean = plan if level == 3 else mean_ref[places_ref[level, s]]
            out_ref[s, part, :] = mult_ref[s, part, :] + 0.5 * (plan - mean)


def spread(places, full, plan_t, mult_t, nodes):
    vmem = pl.BlockSpec(memory_space=pltpu.VMEM)
    return pl.pallas_call(
        functools.partial(spread_kernel, nodes),
        in_specs=[pl.BlockSpec(memory_space=pltpu.SMEM), vmem, vmem, vmem],
        out_specs=vmem,
        out_shape=jax.ShapeDtypeStruct(plan_t.shape, jnp.float32),
        scratch_shapes=[pltpu.VMEM((nodes, plan_t.shape[1] // 4, plan_t.shape[2]), jnp.float32)],
        compiler_params=pltpu.CompilerParams(vmem_limit_bytes=24 * 2**20),
        name="spread",
    )(places, full, plan_t, mult_t)


def per_device(
    demand,
    tariff,
    feeder_price,
    multiplier,
    previous_mean,
    inverse,
    power_limit,
    weights,
    tree_node,
    building_feeder,
    feeder_limit,
):
    slot_count = demand.shape[2]
    section_len = slot_count // 4
    iterate, partial_load = prox(
        demand, tariff, feeder_price, multiplier, previous_mean, inverse, power_limit, building_feeder
    )
    plan_t = jnp.transpose(iterate, (0, 2, 1))
    mult_t = jnp.transpose(multiplier, (0, 2, 1))
    devices = lax.axis_size("scen")
    fine_count = devices * demand.shape[0] // 8
    offsets = jnp.array([[1], [1 + COARSE]], jnp.int32)
    places = jnp.concatenate([jnp.zeros_like(tree_node[:1]), tree_node + offsets], axis=0)
    nodes = 1 + COARSE + fine_count
    hits = places[:, None, :] == jnp.arange(nodes)[None, :, None]
    weighted = jnp.sum(hits.astype(jnp.float32), axis=0) * weights[None, :]
    local = node_sums(weighted, plan_t, section_len, devices)
    full, feeder_load = exchange(local, partial_load)
    new_multiplier = jnp.transpose(spread(places, full, plan_t, mult_t, nodes), (0, 2, 1))
    feeder_load = jnp.transpose(feeder_load, (1, 0, 2))
    new_price = jnp.maximum(0.0, feeder_price + (feeder_load - feeder_limit[None, :, :]) / FEED)
    return (iterate, new_multiplier, new_price)


def solution(mesh):
    in_specs = (
        P("scen", "bldg", None),
        P("scen", None),
        P("scen", None, None),
        P("scen", "bldg", None),
        P("scen", "bldg", None),
        P("bldg", None, None),
        P("bldg", None),
        P("scen"),
        P(None, "scen"),
        P("bldg"),
        P(),
    )
    out_specs = (P("scen", "bldg", None), P("scen", "bldg", None), P("scen", None, None))
    return jax.shard_map(
        per_device, mesh=mesh, in_specs=in_specs, out_specs=out_specs, check_vma=False
    )
```

profile of v0, /device:TPU:0, one launch (start us, length us, event | category | flops | bytes accessed | tf_op | source)
XLA Modules:
  0.0 88.4 jit_solution(10433568436858692122)
XLA Ops:
  0.6 11.6 %copy.37.inv_ref = f32[256,96,96]{2,1,0:T(8,128)} copy(f32[256,96,96]{0,2,1:T(8,128)} %param.17) | data formatting | bytes 18874368 | tf_op args[5]
  12.2 1.8 %copy.34.demand_ref = f32[16,256,96]{2,1,0:T(8,128)S(1)} copy(f32[16,256,96]{1,2,0:T(8,128)} %param.12) | data formatting | bytes 3145728 | tf_op args[0]
  14.1 2.8 %copy.35.mult_ref = f32[16,256,96]{2,1,0:T(8,128)} copy(f32[16,256,96]{1,2,0:T(8,128)} %param.15) | data formatting | bytes 3145728 | tf_op args[3]
  16.9 0.0 copy-start.8
  16.9 0.0 copy-start.5
  16.9 0.0 copy-start.6
  16.9 0.0 copy-start.7
  16.9 2.8 %copy.36.prev_ref = f32[16,256,96]{2,1,0:T(8,128)} copy(f32[16,256,96]{1,2,0:T(8,128)} %param.16) | data formatting | bytes 3145728 | tf_op args[4]
  19.7 0.0 copy-done.8
  19.7 0.1 copy.38.limit_ref
  19.8 0.0 copy-done.5
  19.8 0.0 copy-done.6
  19.8 0.0 copy-done.7
  19.8 0.0 copy-start.1
  19.8 1.6 %copy-done.1 = f32[16,256,96]{2,1,0:T(8,128)S(1)} copy-done((f32[16,256,96]{2,1,0:T(8,128)S(1)}, f32[16,256,96]{2,1,0:T(8,128)}, u32[]{:S(2)}) %copy-start.1) | copy-done | bytes 1572888
  21.4 0.0 copy-start.2
  21.4 1.6 %copy-done.2 = f32[16,256,96]{2,1,0:T(8,128)S(1)} copy-done((f32[16,256,96]{2,1,0:T(8,128)S(1)}, f32[16,256,96]{2,1,0:T(8,128)}, u32[]{:S(2)}) %copy-start.2) | copy-done | bytes 1572888
  23.0 35.0 %prox.1 = (f32[16,256,96]{2,1,0:T(8,128)S(1)}, f32[8,16,96]{2,1,0:T(8,128)S(1)}) custom-call(f32[16,256,96]{2,1,0:T(8,128)S(1)} %copy.34.demand_ref, f32[16,96]{1,0:T(8,128)S(1)} %copy-done.6, f32[16,8,96]{2,1,0:T(8,128)S(1)} %copy-done.5, f32[16,256,96]{2,1,0:T(8,128)S(1)} %copy-done.1, f32[16,256,96]{2,1,0:T(8,128)S(1)} %copy-done.2, ...), custom_call_target="tpu_custom_call" | custom-call | tf_op jit(solution)/shard_map/prox/pallas_call | solution.py:71
  58.0 0.0 copy-start.4
  58.0 1.3 %copy-done.4 = f32[16,256,96]{2,1,0:T(8,128)} copy-done((f32[16,256,96]{2,1,0:T(8,128)}, f32[16,256,96]{2,1,0:T(8,128)S(1)}, u32[]{:S(2)}) %copy-start.4) | copy-done | bytes 1572888
  59.3 0.0 copy-start.10
  59.3 0.0 copy-start.12
  59.3 0.0 copy-start.11
  59.3 1.9 %copy.43 = f32[16,256,96]{1,2,0:T(8,128)S(1)} copy(f32[16,256,96]{2,1,0:T(8,128)} %copy-done.4) | data formatting | bytes 3145728
  61.3 0.0 copy-start
  61.3 0.0 copy-start.3
  61.3 0.0 copy-done.10
  61.3 0.0 copy-done.12
  61.3 0.1 broadcast_add_fusion
  61.4 0.1 convert_reduce_fusion
  61.5 0.1 copy.39
  61.6 0.0 copy-done.11
  61.6 1.8 %node_sums.1.sums_ref = f32[640,256]{1,0:T(8,128)S(1)} custom-call(f32[25,16]{1,0:T(8,128)S(1)} %broadcast_multiply_fusion.weighted_ref, f32[16,96,256]{2,1,0:T(8,128)S(1)} %bitcast.7), custom_call_target="tpu_custom_call" | custom-call | tf_op jit(solution)/shard_map/node_sums/pallas_call | solution.py:130
  63.4 22.0 %exchange.1 = (f32[640,256]{1,0:T(8,128)S(1)}, f32[8,16,96]{2,1,0:T(8,128)S(1)}) custom-call(f32[640,256]{1,0:T(8,128)S(1)} %node_sums.1.sums_ref, f32[8,16,96]{2,1,0:T(8,128)S(1)} %get-tuple-element.8.load_ref), custom_call_target="tpu_custom_call" | custom-call | tf_op jit(solution)/shard_map/exchange/pallas_call | solution.py:209
  85.4 0.0 copy-done.3
  85.4 0.0 copy-start.9
  85.4 2.3 %spread.1 = f32[16,96,256]{2,1,0:T(8,128)} custom-call(s32[3,16]{1,0:T(4,128)S(1)} %concatenate.3.places_ref, f32[640,256]{1,0:T(8,128)S(1)} %get-tuple-element.9.full_ref, f32[16,96,256]{2,1,0:T(8,128)S(1)} %bitcast.8, f32[16,96,256]{2,1,0:T(8,128)S(1)} %bitcast.9), custom_call_target="tpu_custom_call" | custom-call | tf_op jit(solution)/shard_map/spread/pallas_call | solution.py:254
  87.7 0.0 copy-done
  87.7 0.0 copy-done.9
  87.7 0.7 copy.44
  (3 shorter events, 0.0 us)
Async XLA Ops:
  16.9 2.9 %copy-start.8 = (f32[256,96]{0,1:T(8,128)S(1)}, f32[256,96]{0,1:T(8,128)}, u32[]{:S(2)}) copy-start(f32[256,96]{0,1:T(8,128)} %param.18) | copy-start | bytes 294916
  16.9 3.0 %copy-start.5 = (f32[16,8,96]{2,1,0:T(8,128)S(1)}, f32[16,8,96]{2,1,0:T(8,128)}, u32[]{:S(2)}) copy-start(f32[16,8,96]{2,1,0:T(8,128)} %price_ref.1) | copy-start | bytes 147460
  16.9 3.0 %copy-start.6 = (f32[16,96]{1,0:T(8,128)S(1)}, f32[16,96]{1,0:T(8,128)}, u32[]{:S(2)}) copy-start(f32[16,96]{1,0:T(8,128)} %tariff_ref.1) | copy-start | bytes 18436
  16.9 3.0 %copy-start.7 = (s32[256]{0:T(256)S(1)}, s32[256]{0:T(256)}, u32[]{:S(2)}) copy-start(s32[256]{0:T(256)} %feeder_ref.1) | copy-start | bytes 3076
  19.8 1.6 %copy-start.1 = (f32[16,256,96]{2,1,0:T(8,128)S(1)}, f32[16,256,96]{2,1,0:T(8,128)}, u32[]{:S(2)}) copy-start(f32[16,256,96]{2,1,0:T(8,128)} %copy.35.mult_ref) | copy-start | bytes 4718596
  21.4 1.6 %copy-start.2 = (f32[16,256,96]{2,1,0:T(8,128)S(1)}, f32[16,256,96]{2,1,0:T(8,128)}, u32[]{:S(2)}) copy-start(f32[16,256,96]{2,1,0:T(8,128)} %copy.36.prev_ref) | copy-start | bytes 4718596
  58.0 1.3 %copy-start.4 = (f32[16,256,96]{2,1,0:T(8,128)}, f32[16,256,96]{2,1,0:T(8,128)S(1)}, u32[]{:S(2)}) copy-start(f32[16,256,96]{2,1,0:T(8,128)S(1)} %get-tuple-element.17) | copy-start | bytes 4718596
  59.3 2.0 %copy-start.10 = (s32[2,16]{1,0:T(2,128)S(1)}, s32[2,16]{1,0:T(2,128)}, u32[]{:S(2)}) copy-start(s32[2,16]{1,0:T(2,128)} %param.20) | copy-start | bytes 388
  59.3 2.0 %copy-start.12 = (s32[2]{0:T(128)S(1)}, s32[2]{0:T(128)}, u32[]{:S(2)}) copy-start(s32[2]{0:T(128)} %constant.13) | copy-start | bytes 28
  59.3 2.2 %copy-start.11 = (f32[16]{0:T(128)S(1)}, f32[16]{0:T(128)}, u32[]{:S(2)}) copy-start(f32[16]{0:T(128)} %param.19) | copy-start | bytes 196
  61.3 26.4 %copy-start = (f32[16,256,96]{1,2,0:T(8,128)}, f32[16,256,96]{1,2,0:T(8,128)S(1)}, u32[]{:S(2)}) copy-start(f32[16,256,96]{1,2,0:T(8,128)S(1)} %copy.43) | copy-start | bytes 4718596
  61.3 24.1 %copy-start.3 = (f32[16,256,96]{1,2,0:T(8,128)S(1)}, f32[16,256,96]{1,2,0:T(8,128)}, u32[]{:S(2)}) copy-start(f32[16,256,96]{1,2,0:T(8,128)} %param.15) | copy-start | bytes 4718596
  85.4 2.3 %copy-start.9 = (f32[8,96]{1,0:T(8,128)S(1)}, f32[8,96]{1,0:T(8,128)}, u32[]{:S(2)}) copy-start(f32[8,96]{1,0:T(8,128)} %param.22) | copy-start | bytes 9220
where the time goes:
time: 90 us; the launch traced here: 88.4 us
  Pallas kernels  61 us (68%)
  local copies, waits for them, and re-layouts  26.4 us (29%)
    pallas_call x1, Pallas kernels, prox(): pl.pallas_call(prox_kernel, grid=(count // block,), in_specs=[big, whole2...  35 us
    unnamed x33, local copies, waits for them, and re-layouts  26.3 us
    pallas_call x1, Pallas kernels, exchange(): pl.pallas_call(functools.partial(exchange_kernel, scen_size, bldg_size),...  22 us
    pallas_call x1, Pallas kernels, spread(): pl.pallas_call(functools.partial(spread_kernel, nodes), in_specs=[pl.Bloc...  2.28 us

commit v1 on v0

v1 whole, which is shorter than its diff:
```python
import functools

import jax
import jax.numpy as jnp
from jax import lax
from jax.experimental import pallas as pl
from jax.experimental.pallas import tpu as pltpu
from jax.sharding import PartitionSpec as P

FEED = 128
PROX = 12
COARSE = 8
LANES = 128
MESH = pl.DeviceIdType.MESH
BF16 = jnp.bfloat16
F32 = jnp.float32


def round_up(value, unit):
    return (value + unit - 1) // unit * unit


def split3(value):
    first = value.astype(BF16)
    rest = value - first.astype(F32)
    second = rest.astype(BF16)
    third = (rest - second.astype(F32)).astype(BF16)
    return first, second, third


def share_kernel(
    pieces, demand_hbm, mult_hbm, prev_hbm, tariff_ref, price_ref, limit_ref, feeder_ref, weight_ref, tree_ref,
    keep_ref, got_ref, table_ref,
    demand, mult, prev, send, landed, table, table_landed, hot,
    load_sem, send_sem, recv_sem, table_send, table_recv,
):
    scen, slots, count = demand.shape
    half = count // 2
    each = scen // pieces
    feeders = price_ref.shape[1]
    me, column = lax.axis_index("scen"), lax.axis_index("bldg")
    core = lax.rem(me, 2)
    partner = (me + 1 - 2 * core, column)
    loads = []
    for p in range(pieces):
        rows = pl.ds(p * each, each)
        group = []
        for k, (src, dst) in enumerate(((demand_hbm, demand), (mult_hbm, mult), (prev_hbm, prev))):
            copy = pltpu.make_async_copy(src.at[rows], dst.at[rows], load_sem.at[p, k])
            copy.start()
            group.append(copy)
        loads.append(group)
    barrier = pltpu.get_barrier_semaphore()
    pl.semaphore_signal(barrier, inc=1, device_id=partner, device_id_type=MESH)

    nodes = table.shape[0]
    row = lax.broadcasted_iota(jnp.int32, (nodes, scen), 0)
    first = tree_ref[0:1, :] + 1
    second = tree_ref[1:2, :] + (1 + COARSE)
    hit = (row == 0) | (row == first) | (row == second)
    table[...] = jnp.where(hit, weight_ref[...], 0.0)
    table_ref[0] = table[...]
    one = lax.broadcasted_iota(jnp.int32, (feeders, count), 0) == feeder_ref[...]
    one = one.astype(F32).astype(BF16)
    for k in range(3):
        hot[k * feeders : (k + 1) * feeders, :] = one

    pl.semaphore_wait(barrier, 1)
    table_copy = pltpu.make_async_remote_copy(
        src_ref=table, dst_ref=table_landed, send_sem=table_send, recv_sem=table_recv,
        device_id=partner, device_id_type=MESH,
    )
    table_copy.start()

    def fill(s, offset, into):
        lanes = pl.ds(pl.multiple_of(offset, LANES), half)
        price = price_ref[s] + tariff_ref[pl.ds(s, 1), :]
        terms = jnp.concatenate(split3(price), axis=0)
        local = lax.dot_general(terms, hot[:, lanes], (((0,), (0,)), ((), ())), preferred_element_type=F32)
        before = prev[s, :, lanes]
        into[0, s] = 0.5 * before - (local - demand[s, :, lanes]) - mult[s, :, lanes]
        into[1, s] = jnp.clip(before, 0.0, limit_ref[:, lanes])

    copies = []
    for p in range(pieces):
        for copy in loads[p]:
            copy.wait()
        for s in range(p * each, (p + 1) * each):
            fill(s, half - core * half, send)
        rows = pl.ds(p * each, each)
        copy = pltpu.make_async_remote_copy(
            src_ref=send.at[:, rows], dst_ref=landed.at[:, rows],
            send_sem=send_sem.at[p], recv_sem=recv_sem.at[p],
            device_id=partner, device_id_type=MESH,
        )
        copy.start()
        copies.append(copy)
    for s in range(scen):
        fill(s, core * half, keep_ref)
    table_copy.wait()
    table_ref[1] = table_landed[...]
    for p in range(pieces):
        copies[p].wait_recv()
        rows = pl.ds(p * each, each)
        got_ref[:, rows] = landed[:, rows]
    for copy in copies:
        copy.wait_send()


def share(demand, mult, prev, tariff, price, limit, feeder, weights, tree, nodes):
    scen, slots, count = demand.shape
    feeders = price.shape[1]
    half = count // 2
    pieces = 4
    vmem = pl.BlockSpec(memory_space=pltpu.VMEM)
    hbm = pl.BlockSpec(memory_space=pl.ANY)
    dma = pltpu.SemaphoreType.DMA
    pair = (2, scen, slots, half)
    return pl.pallas_call(
        functools.partial(share_kernel, pieces),
        in_specs=[hbm, hbm, hbm] + [vmem] * 6,
        out_specs=[vmem, vmem, vmem],
        out_shape=[
            jax.ShapeDtypeStruct(pair, F32),
            jax.ShapeDtypeStruct(pair, F32),
            jax.ShapeDtypeStruct((2, nodes, scen), F32),
        ],
        scratch_shapes=[
            pltpu.VMEM(demand.shape, F32), pltpu.VMEM(demand.shape, F32), pltpu.VMEM(demand.shape, F32),
            pltpu.VMEM(pair, F32), pltpu.VMEM(pair, F32),
            pltpu.VMEM((nodes, scen), F32), pltpu.VMEM((nodes, scen), F32),
            pltpu.VMEM((3 * feeders, count), BF16),
            dma((pieces, 3)), dma((pieces,)), dma((pieces,)), dma(()), dma(()),
        ],
        compiler_params=pltpu.CompilerParams(
            collective_id=1, has_side_effects=True, vmem_limit_bytes=40 * 2**20
        ),
        name="share",
    )(demand, mult, prev, tariff, price, limit, feeder, weights, tree)


def prox_kernel(
    nodes, pieces, inv_hbm, limit_ref, feeder_ref, keep_ref, got_ref, table_ref,
    mine_ref, theirs_ref, sums_ref, load_ref,
    inv, w_ref, fixed_ref, z_ref, u_ref, both_ref, cap_ref, inv_sem,
):
    slots, _, half = inv.shape
    _, scen, _, _ = keep_ref.shape
    wide = 2 * scen
    feeders = load_ref.shape[1]
    core = lax.rem(lax.axis_index("scen"), 2)
    lanes = pl.ds(pl.multiple_of(core * half, LANES), half)
    each = slots // pieces

    def inv_copy(p):
        rows = pl.ds(p * each, each)
        return pltpu.make_async_copy(inv_hbm.at[rows, :, lanes], inv.at[rows], inv_sem.at[p])

    for p in range(pieces):
        inv_copy(p).start()
    cap_ref[...] = jnp.transpose(limit_ref[:, lanes], (1, 0))

    for k, source in enumerate((keep_ref, got_ref)):
        part = slice(k * scen, (k + 1) * scen)
        fixed = jnp.transpose(source[0], (2, 0, 1))
        start = jnp.transpose(source[1], (2, 0, 1))
        right = start + fixed
        high = right.astype(BF16)
        fixed_ref[:, part, :] = fixed
        both_ref[:, part, :] = high
        both_ref[:, wide + k * scen : wide + (k + 1) * scen, :] = (right - high.astype(F32)).astype(BF16)
    u_ref[...] = jnp.zeros_like(u_ref)

    for p in range(pieces):
        inv_copy(p).wait()
        rows = slice(p * each, (p + 1) * each)
        full = jnp.transpose(inv[rows], (2, 0, 1))
        high = full.astype(BF16)
        w_ref[:, rows, :slots] = high
        w_ref[:, rows, LANES : LANES + slots] = (full - high.astype(F32)).astype(BF16)

    def iteration(i, carry):
        for b in range(half):
            out = jnp.dot(both_ref[b], w_ref[b], preferred_element_type=F32)
            primal = out[:wide, :slots] + (out[:wide, LANES : LANES + slots] + out[wide:, :slots])
            moved = primal + u_ref[b]
            fresh = jnp.clip(moved, 0.0, cap_ref[b : b + 1, :])
            dual = moved - fresh
            right = fresh - dual + fixed_ref[b]
            high = right.astype(BF16)
            z_ref[b] = fresh
            u_ref[b] = dual
            both_ref[b, :wide] = high
            both_ref[b, wide:] = (right - high.astype(F32)).astype(BF16)
        return carry

    lax.fori_loop(0, PROX, iteration, 0)

    mine_ref[...] = jnp.transpose(z_ref[:, :scen, :], (1, 2, 0))
    theirs_ref[...] = jnp.transpose(z_ref[:, scen:, :], (1, 2, 0))

    length = slots // 4
    tail = nodes * length
    rest = sums_ref.shape[0] - tail
    sums_ref[pl.ds(tail, rest), :] = jnp.zeros((rest, half), F32)
    plans = (mine_ref, theirs_ref)

    def add_nodes(level, at_once):
        part = slice(level * length, (level + 1) * length)

        def body(step, base):
            first = base + step * at_once
            totals = [0.0] * at_once
            accs = [jnp.zeros((length, half), F32)] * at_once
            for k in range(2):
                for s in range(scen):
                    block = plans[k][s, part, :]
                    for j in range(at_once):
                        factor = table_ref[k, first + j, s]
                        totals[j] = totals[j] + factor
                        accs[j] = accs[j] + factor * block
            for j in range(at_once):
                sums_ref[pl.ds(pl.multiple_of((first + j) * length, 8), length), :] = accs[j]
                sums_ref[pl.ds(tail + first + j, 1), :] = jnp.full((1, half), totals[j], F32)
            return base

        return body

    add_nodes(0, 1)(0, 0)
    lax.fori_loop(0, COARSE // 4, add_nodes(1, 4), 1)
    lax.fori_loop(0, (nodes - 1 - COARSE) // 4, add_nodes(2, 4), 1 + COARSE)

    one = lax.broadcasted_iota(jnp.int32, (feeders, half), 0) == feeder_ref[:, lanes]
    one = one.astype(F32).astype(BF16)
    for k in range(2):
        for s in range(scen):
            value = plans[k][s]
            high = value.astype(BF16)
            low = (value - high.astype(F32)).astype(BF16)
            dims = (((1,), (1,)), ((), ()))
            load_ref[k * scen + s] = lax.dot_general(
                one, high, dims, preferred_element_type=F32
            ) + lax.dot_general(one, low, dims, preferred_element_type=F32)


def prox(inverse, limit, feeder, keep, got, table, nodes, feeders, rows):
    slots, _, count = inverse.shape
    _, scen, _, half = keep.shape
    pieces = slots // 16
    vmem = pl.BlockSpec(memory_space=pltpu.VMEM)
    plan = jax.ShapeDtypeStruct((scen, slots, half), F32)
    state = pltpu.VMEM((half, 2 * scen, slots), F32)
    return pl.pallas_call(
        functools.partial(prox_kernel, nodes, pieces),
        in_specs=[
            pl.BlockSpec(memory_space=pl.ANY), vmem, vmem, vmem, vmem,
            pl.BlockSpec(memory_space=pltpu.SMEM),
        ],
        out_specs=[vmem] * 4,
        out_shape=[
            plan, plan,
            jax.ShapeDtypeStruct((rows, half), F32),
            jax.ShapeDtypeStruct((2 * scen, feeders, slots), F32),
        ],
        scratch_shapes=[
            pltpu.VMEM((slots, slots, half), F32),
            pltpu.VMEM((half, slots, 2 * LANES), BF16),
            state, state, state,
            pltpu.VMEM((half, 4 * scen, slots), BF16),
            pltpu.VMEM((half, slots), F32),
            pltpu.SemaphoreType.DMA((pieces,)),
        ],
        compiler_params=pltpu.CompilerParams(vmem_limit_bytes=50 * 2**20),
        name="prox",
    )(inverse, limit, feeder, keep, got, table)


def exchange_kernel(
    scen_size, bldg_size, sums_ref, theirs_ref, load_ref,
    full_ref, back_ref, total_ref,
    landed, own, whole, other, plan_landed, load_first, load_mine, load_landed,
    rs_send, rs_recv, ag_send, ag_recv, on_send, on_recv, plan_send, plan_recv, pair_send, pair_recv, load_send, load_recv,
):
    chips = scen_size // 2
    me, column = lax.axis_index("scen"), lax.axis_index("bldg")
    core = lax.rem(me, 2)
    chip = lax.div(me, 2)
    chunk, half = own.shape
    scen = total_ref.shape[0]
    partner = (me + 1 - 2 * core, column)
    peers = [(lax.rem(me + 2 * k, scen_size), column) for k in range(1, chips)]
    beside = [(me, lax.rem(column + k, bldg_size)) for k in range(1, bldg_size)]
    barrier = pltpu.get_barrier_semaphore()
    for peer in [partner] + peers + beside:
        pl.semaphore_signal(barrier, inc=1, device_id=peer, device_id_type=MESH)
    pl.semaphore_wait(barrier, chips + bldg_size - 1)

    def rows_of(index):
        return pl.ds(pl.multiple_of(index * chunk, 8), chunk)

    def remote(src, dst, send_sem, recv_sem, device):
        copy = pltpu.make_async_remote_copy(
            src_ref=src, dst_ref=dst, send_sem=send_sem, recv_sem=recv_sem,
            device_id=device, device_id_type=MESH,
        )
        copy.start()
        return copy

    scatter = [
        remote(sums_ref.at[rows_of(lax.div(peer[0], 2))], landed.at[k], rs_send.at[k], rs_recv.at[k], peer)
        for k, peer in enumerate(peers)
    ]
    pair_load = remote(load_ref.at[pl.ds(scen, scen)], load_first, pair_send, pair_recv, partner)
    plan_copy = remote(theirs_ref, plan_landed, plan_send, plan_recv, partner)

    pair_load.wait_recv()
    load_mine[...] = load_ref[pl.ds(0, scen)] + load_first[...]
    loads = [
        remote(load_mine, load_landed.at[k], load_send.at[k], load_recv.at[k], peer)
        for k, peer in enumerate(beside)
    ]

    for copy in scatter:
        copy.wait_recv()
    acc = sums_ref[rows_of(chip), :]
    for k in range(chips - 1):
        acc = acc + landed[k]
    own[...] = acc
    gather = [
        remote(own, whole.at[k + 1], ag_send.at[k], ag_recv.at[k], peer)
        for k, peer in enumerate(peers)
    ]
    onward = [remote(own, other.at[0], on_send.at[0], on_recv.at[0], partner)]
    lanes = pl.ds(pl.multiple_of(core * half, LANES), half)
    full_ref[rows_of(chip), lanes] = acc

    total = load_mine[...]
    for k, copy in enumerate(loads):
        copy.wait_recv()
        total = total + load_landed[k]
    total_ref[...] = total
    plan_copy.wait_recv()
    back_ref[...] = plan_landed[...]

    for k in range(1, chips):
        gather[k - 1].wait_recv()
        onward.append(remote(whole.at[k], other.at[k], on_send.at[k], on_recv.at[k], partner))
        source = lax.rem(chip - k + chips, chips)
        full_ref[rows_of(source), lanes] = whole[k]
    away = pl.ds(pl.multiple_of(half - core * half, LANES), half)
    for k in range(chips):
        onward[k].wait_recv()
        source = lax.rem(chip - k + chips, chips)
        full_ref[rows_of(source), away] = other[k]
    for copy in scatter + [pair_load, plan_copy] + loads + gather + onward:
        copy.wait_send()


def exchange(sums, theirs, load):
    scen_size, bldg_size = lax.axis_size("scen"), lax.axis_size("bldg")
    chips = scen_size // 2
    rows, half = sums.shape
    chunk = rows // chips
    dma = pltpu.SemaphoreType.DMA
    vmem = pl.BlockSpec(memory_space=pltpu.VMEM)
    mine = (load.shape[0] // 2,) + load.shape[1:]
    return pl.pallas_call(
        functools.partial(exchange_kernel, scen_size, bldg_size),
        in_specs=[vmem] * 3,
        out_specs=[vmem] * 3,
        out_shape=[
            jax.ShapeDtypeStruct((rows, 2 * half), F32),
            jax.ShapeDtypeStruct(theirs.shape, F32),
            jax.ShapeDtypeStruct(mine, F32),
        ],
        scratch_shapes=[
            pltpu.VMEM((chips - 1, chunk, half), F32),
            pltpu.VMEM((chunk, half), F32),
            pltpu.VMEM((chips, chunk, half), F32),
            pltpu.VMEM((chips, chunk, half), F32),
            pltpu.VMEM(theirs.shape, F32),
            pltpu.VMEM(mine, F32),
            pltpu.VMEM(mine, F32),
            pltpu.VMEM((bldg_size - 1,) + mine, F32),
            dma((chips - 1,)), dma((chips - 1,)),
            dma((chips - 1,)), dma((chips - 1,)),
            dma((chips,)), dma((chips,)),
            dma(()), dma(()), dma(()), dma(()),
            dma((bldg_size - 1,)), dma((bldg_size - 1,)),
        ],
        compiler_params=pltpu.CompilerParams(
            collective_id=0, has_side_effects=True, vmem_limit_bytes=24 * 2**20
        ),
        name="exchange",
    )(sums, theirs, load)


def spread_kernel(
    nodes, tree_ref, full_ref, mine_ref, back_ref, mult_ref, price_ref, load_ref, limit_ref,
    plan_ref, out_ref, new_price_ref, mean_ref,
):
    step = pl.program_id(0)
    each, slots, count = mult_ref.shape
    half = count // 2
    length = slots // 4
    tail = nodes * length
    core = lax.rem(lax.axis_index("scen"), 2)

    @pl.when(step == 0)
    def _():
        def divide(n, carry):
            share = full_ref[pl.ds(pl.multiple_of(n * length, 8), length), :]
            mean_ref[n] = share / full_ref[pl.ds(tail + n, 1), :]
            return carry

        lax.fori_loop(0, nodes, divide, 0)

    for j in range(each):
        s = step * each + j
        places = (0, tree_ref[0, s] + 1, tree_ref[1, s] + (1 + COARSE))
        for source, offset in ((mine_ref, core * half), (back_ref, half - core * half)):
            lanes = pl.ds(pl.multiple_of(offset, LANES), half)
            plan_ref[j, :, lanes] = source[j]
            for level in range(4):
                part = slice(level * length, (level + 1) * length)
                plan = source[j, part, :]
                mean = plan if level == 3 else mean_ref[places[level], :, lanes]
                out_ref[j, part, lanes] = mult_ref[j, part, lanes] + 0.5 * (plan - mean)
    new_price_ref[...] = jnp.maximum(0.0, price_ref[...] + (load_ref[...] - limit_ref[...][None]) / FEED)


def spread(tree, full, mine, back, mult, price, load, limit, nodes):
    scen, slots, count = mult.shape
    feeders = price.shape[1]
    each = 4
    block = lambda *shape: pl.BlockSpec((each,) + shape, lambda i: (i, 0, 0))
    return pl.pallas_call(
        functools.partial(spread_kernel, nodes),
        grid=(scen // each,),
        in_specs=[
            pl.BlockSpec(memory_space=pltpu.SMEM),
            pl.BlockSpec(full.shape, lambda i: (0, 0)),
            block(slots, count // 2), block(slots, count // 2), block(slots, count),
            block(feeders, slots), block(feeders, slots),
            pl.BlockSpec(limit.shape, lambda i: (0, 0)),
        ],
        out_specs=[block(slots, count), block(slots, count), block(feeders, slots)],
        out_shape=[
            jax.ShapeDtypeStruct(mult.shape, F32),
            jax.ShapeDtypeStruct(mult.shape, F32),
            jax.ShapeDtypeStruct(price.shape, F32),
        ],
        scratch_shapes=[pltpu.VMEM((nodes, slots // 4, count), F32)],
        compiler_params=pltpu.CompilerParams(vmem_limit_bytes=24 * 2**20),
        name="spread",
    )(tree, full, mine, back, mult, price, load, limit)


def per_device(
    demand,
    tariff,
    feeder_price,
    multiplier,
    previous_mean,
    inverse,
    power_limit,
    weights,
    tree_node,
    building_feeder,
    feeder_limit,
):
    scen_size = lax.axis_size("scen")
    scen, count, slots = demand.shape
    feeders = feeder_price.shape[1]
    nodes = 1 + COARSE + scen_size * scen // 8
    rows = round_up(nodes * (slots // 4) + nodes, 8 * (scen_size // 2))

    def turned(value):
        return jnp.transpose(value, (0, 2, 1))

    limit = jnp.transpose(power_limit, (1, 0))
    feeder = building_feeder.reshape(1, count)
    mult = turned(multiplier)
    keep, got, table = share(
        turned(demand), mult, turned(previous_mean), tariff, feeder_price, limit, feeder,
        weights.reshape(1, scen), tree_node, nodes,
    )
    mine, theirs, sums, load = prox(
        jnp.transpose(inverse, (1, 2, 0)), limit, feeder, keep, got, table, nodes, feeders, rows
    )
    full, back, total = exchange(sums, theirs, load)
    plan, new_multiplier, new_price = spread(
        tree_node, full, mine, back, mult, feeder_price, total, feeder_limit, nodes
    )
    return turned(plan), turned(new_multiplier), new_price


def solution(mesh):
    in_specs = (
        P("scen", "bldg", None),
        P("scen", None),
        P("scen", None, None),
        P("scen", "bldg", None),
        P("scen", "bldg", None),
        P("bldg", None, None),
        P("bldg", None),
        P("scen"),
        P(None, "scen"),
        P("bldg"),
        P(),
    )
    out_specs = (P("scen", "bldg", None), P("scen", "bldg", None), P("scen", None, None))
    return jax.shard_map(
        per_device, mesh=mesh, in_specs=in_specs, out_specs=out_specs, check_vma=False
    )
```

time: 90 us -> 62.2 us (0.69); the launches traced: 88.4 us -> 61.8 us
  local copies, waits for them, and re-layouts: 26.4 us -> 9.82 us
  Pallas kernels: 61 us -> 51.3 us
    unnamed x33 -> x32, local copies, waits for them, and re-layouts: 26.3 us -> 9.82 us
    pallas_call x1, Pallas kernels: 22 us -> 17.1 us  [exchange(): pl.pallas_call(functools.partial(exchange_kernel, scen_size, bldg_size),...]
    pallas_call x3, Pallas kernels: 39 us -> 34.2 us  [the longest x1 24.9 us: prox(): pl.pallas_call(functools.partial(prox_kernel, nodes, pieces), in_specs=[p...]
where the time goes in v1:
time: 62.2 us; the launch traced here: 61.8 us
  Pallas kernels  51.3 us (82%)
  local copies, waits for them, and re-layouts  9.82 us (16%)
  between operations  0.74 us (1%)
    pallas_call x1, Pallas kernels, prox(): pl.pallas_call(functools.partial(prox_kernel, nodes, pieces), in_specs=[p...  24.9 us
    pallas_call x1, Pallas kernels, exchange(): pl.pallas_call(functools.partial(exchange_kernel, scen_size, bldg_size),...  17.1 us
    unnamed x32, local copies, waits for them, and re-layouts  9.82 us
    pallas_call x1, Pallas kernels, share(): pl.pallas_call(functools.partial(share_kernel, pieces), in_specs=[hbm, hb...  6.19 us
    pallas_call x1, Pallas kernels, spread(): pl.pallas_call(functools.partial(spread_kernel, nodes), grid=(scen // eac...  3.05 us

profile of v1, /device:TPU:0, one launch (start us, length us, event | category | flops | bytes accessed | tf_op | source)
XLA Modules:
  0.0 61.8 jit_solution(7882146240524347913)
XLA Ops:
  0.6 0.0 copy-start
  0.6 1.4 %copy-done = f32[16,256,96]{1,2,0:T(8,128)S(1)} copy-done((f32[16,256,96]{1,2,0:T(8,128)S(1)}, f32[16,256,96]{1,2,0:T(8,128)}, u32[]{:S(2)}) %copy-start) | copy-done | bytes 1572888
  2.0 0.0 copy-start.3
  2.0 1.4 %copy-done.3 = f32[16,256,96]{1,2,0:T(8,128)S(1)} copy-done((f32[16,256,96]{1,2,0:T(8,128)S(1)}, f32[16,256,96]{1,2,0:T(8,128)}, u32[]{:S(2)}) %copy-start.3) | copy-done | bytes 1572888
  3.5 0.0 copy-start.4
  3.5 1.4 %copy-done.4 = f32[16,256,96]{1,2,0:T(8,128)S(1)} copy-done((f32[16,256,96]{1,2,0:T(8,128)S(1)}, f32[16,256,96]{1,2,0:T(8,128)}, u32[]{:S(2)}) %copy-start.4) | copy-done | bytes 1572888
  4.9 0.0 copy-start.5
  4.9 0.9 %copy-done.5 = f32[256,96]{0,1:T(8,128)S(1)} copy-done((f32[256,96]{0,1:T(8,128)S(1)}, f32[256,96]{0,1:T(8,128)}, u32[]{:S(2)}) %copy-start.5) | copy-done | bytes 98328
  5.8 0.0 copy-start.7
  5.8 0.8 %copy-done.7 = f32[16,8,96]{2,1,0:T(8,128)S(1)} copy-done((f32[16,8,96]{2,1,0:T(8,128)S(1)}, f32[16,8,96]{2,1,0:T(8,128)}, u32[]{:S(2)}) %copy-start.7) | copy-done | bytes 49176
  6.6 0.0 copy-start.9
  6.6 0.7 %copy-done.9 = f32[16,96]{1,0:T(8,128)S(1)} copy-done((f32[16,96]{1,0:T(8,128)S(1)}, f32[16,96]{1,0:T(8,128)}, u32[]{:S(2)}) %copy-start.9) | copy-done | bytes 6168
  7.3 0.0 copy-start.11
  7.3 0.7 %copy-done.11 = s32[256]{0:T(256)S(1)} copy-done((s32[256]{0:T(256)S(1)}, s32[256]{0:T(256)}, u32[]{:S(2)}) %copy-start.11) | copy-done | bytes 1048
  8.0 0.0 copy-start.13
  8.0 0.7 %copy-done.13 = s32[2,16]{1,0:T(2,128)S(1)} copy-done((s32[2,16]{1,0:T(2,128)S(1)}, s32[2,16]{1,0:T(2,128)}, u32[]{:S(2)}) %copy-start.13) | copy-done | bytes 152
  8.6 0.0 copy-start.15
  8.7 0.7 %copy-done.15 = f32[16]{0:T(128)S(1)} copy-done((f32[16]{0:T(128)S(1)}, f32[16]{0:T(128)}, u32[]{:S(2)}) %copy-start.15) | copy-done | bytes 88
  9.3 0.0 copy-start.6
  9.3 0.0 copy-start.12
  9.3 6.2 %share.1 = (f32[2,16,96,128]{3,2,1,0:T(8,128)S(1)}, f32[2,16,96,128]{3,2,1,0:T(8,128)S(1)}, f32[2,25,16]{2,1,0:T(8,128)S(1)}) custom-call(f32[16,96,256]{2,1,0:T(8,128)S(1)} %bitcast.11, f32[16,96,256]{2,1,0:T(8,128)S(1)} %bitcast.9, f32[16,96,256]{2,1,0:T(8,128)S(1)} %bitcast.12, f32[16,96]{1,0:T(8,128)S(1)} %copy-done.9, f32[16,8,96]{2,1,0:T(8,128)S(1)} %copy-done.7, ...), custom_call_target="tpu_custom_call" | custom-call | tf_op jit(solution)/shard_map/share/pallas_call | solution.py:119
  15.5 0.0 copy-start.2
  15.5 1.1 %copy-done.2 = f32[2,16,96,128]{3,2,1,0:T(8,128)} copy-done((f32[2,16,96,128]{3,2,1,0:T(8,128)}, f32[2,16,96,128]{3,2,1,0:T(8,128)S(1)}, u32[]{:S(2)}) %copy-start.2) | copy-done | bytes 1572888
  16.7 0.0 copy-done.6
  16.7 0.0 copy-done.12
  16.7 0.0 copy-start.1
  16.7 0.0 copy-start.8
  16.7 0.0 copy-start.10
  16.7 0.0 copy-start.14
  16.7 24.9 %prox.1 = (f32[16,96,128]{2,1,0:T(8,128)S(1)}, f32[16,96,128]{2,1,0:T(8,128)S(1)}, f32[640,128]{1,0:T(8,128)S(1)}, f32[32,8,96]{2,1,0:T(8,128)S(1)}) custom-call(f32[96,96,256]{2,1,0:T(8,128)} %bitcast.18, f32[96,256]{1,0:T(8,128)S(1)} %bitcast.14, s32[1,256]{1,0:T(1,128)S(1)} %bitcast.16, f32[2,16,96,128]{3,2,1,0:T(8,128)S(1)} %get-tuple-element.16.keep_ref, ...), custom_call_target="tpu_custom_call" | custom-call | tf_op jit(solution)/shard_map/prox/pallas_call | solution.py:253
  41.6 17.1 %exchange.1 = (f32[640,256]{1,0:T(8,128)S(1)}, f32[16,96,128]{2,1,0:T(8,128)S(1)}, f32[16,8,96]{2,1,0:T(8,128)S(1)}) custom-call(f32[640,128]{1,0:T(8,128)S(1)} %get-tuple-element.19.sums_ref, f32[16,96,128]{2,1,0:T(8,128)S(1)} %get-tuple-element.20.theirs_ref, f32[32,8,96]{2,1,0:T(8,128)S(1)} %get-tuple-element.21.load_ref), custom_call_target="tpu_custom_call" | custom-call | tf_op jit(solution)/shard_map/exchange/pallas_call | solution.py:367
  58.7 0.0 copy-done.1
  58.7 0.0 copy-done.8
  58.8 0.0 copy-done.10
  58.8 0.0 copy-done.14
  58.8 3.0 %spread.1 = (f32[16,96,256]{2,1,0:T(8,128)}, f32[16,96,256]{2,1,0:T(8,128)}, f32[16,8,96]{2,1,0:T(8,128)}) custom-call(s32[2,16]{1,0:T(2,128)S(1)} %copy-done.14, f32[640,256]{1,0:T(8,128)S(1)} %get-tuple-element.22.full_ref, f32[16,96,128]{2,1,0:T(8,128)S(1)} %get-tuple-element.23.mine_ref, f32[16,96,128]{2,1,0:T(8,128)S(1)} %get-tuple-element.24.back_ref, ...), custom_call_target="tpu_custom_call" | custom-call | tf_op jit(solution)/shard_map/spread/pallas_call | solution.py:437
Async XLA Ops:
  0.6 1.4 %copy-start = (f32[16,256,96]{1,2,0:T(8,128)S(1)}, f32[16,256,96]{1,2,0:T(8,128)}, u32[]{:S(2)}) copy-start(f32[16,256,96]{1,2,0:T(8,128)} %param.14) | copy-start | bytes 4718596
  2.0 1.4 %copy-start.3 = (f32[16,256,96]{1,2,0:T(8,128)S(1)}, f32[16,256,96]{1,2,0:T(8,128)}, u32[]{:S(2)}) copy-start(f32[16,256,96]{1,2,0:T(8,128)} %param.11) | copy-start | bytes 4718596
  3.5 1.4 %copy-start.4 = (f32[16,256,96]{1,2,0:T(8,128)S(1)}, f32[16,256,96]{1,2,0:T(8,128)}, u32[]{:S(2)}) copy-start(f32[16,256,96]{1,2,0:T(8,128)} %param.15) | copy-start | bytes 4718596
  4.9 0.9 %copy-start.5 = (f32[256,96]{0,1:T(8,128)S(1)}, f32[256,96]{0,1:T(8,128)}, u32[]{:S(2)}) copy-start(f32[256,96]{0,1:T(8,128)} %param.17) | copy-start | bytes 294916
  5.8 0.8 %copy-start.7 = (f32[16,8,96]{2,1,0:T(8,128)S(1)}, f32[16,8,96]{2,1,0:T(8,128)}, u32[]{:S(2)}) copy-start(f32[16,8,96]{2,1,0:T(8,128)} %price_ref.3) | copy-start | bytes 147460
  6.6 0.7 %copy-start.9 = (f32[16,96]{1,0:T(8,128)S(1)}, f32[16,96]{1,0:T(8,128)}, u32[]{:S(2)}) copy-start(f32[16,96]{1,0:T(8,128)} %tariff_ref.1) | copy-start | bytes 18436
  7.3 0.7 %copy-start.11 = (s32[256]{0:T(256)S(1)}, s32[256]{0:T(256)}, u32[]{:S(2)}) copy-start(s32[256]{0:T(256)} %param.20) | copy-start | bytes 3076
  8.0 0.7 %copy-start.13 = (s32[2,16]{1,0:T(2,128)S(1)}, s32[2,16]{1,0:T(2,128)}, u32[]{:S(2)}) copy-start(s32[2,16]{1,0:T(2,128)} %tree_ref.3) | copy-start | bytes 388
  8.6 0.7 %copy-start.15 = (f32[16]{0:T(128)S(1)}, f32[16]{0:T(128)}, u32[]{:S(2)}) copy-start(f32[16]{0:T(128)} %param.18) | copy-start | bytes 196
  9.3 7.3 %copy-start.6 = (f32[256,96]{0,1:T(8,128)S(1)}, f32[256,96]{0,1:T(8,128)}, u32[]{:S(2)}) copy-start(f32[256,96]{0,1:T(8,128)} %param.17) | copy-start | bytes 294916
  9.3 7.3 %copy-start.12 = (s32[256]{0:T(256)S(1)}, s32[256]{0:T(256)}, u32[]{:S(2)}) copy-start(s32[256]{0:T(256)} %param.20) | copy-start | bytes 3076
  15.5 1.1 %copy-start.2 = (f32[2,16,96,128]{3,2,1,0:T(8,128)}, f32[2,16,96,128]{3,2,1,0:T(8,128)S(1)}, u32[]{:S(2)}) copy-start(f32[2,16,96,128]{3,2,1,0:T(8,128)S(1)} %get-tuple-element.17.got_ref) | copy-start | bytes 4718596
  16.7 42.1 %copy-start.1 = (f32[16,256,96]{1,2,0:T(8,128)S(1)}, f32[16,256,96]{1,2,0:T(8,128)}, u32[]{:S(2)}) copy-start(f32[16,256,96]{1,2,0:T(8,128)} %param.14) | copy-start | bytes 4718596
  16.7 42.1 %copy-start.8 = (f32[16,8,96]{2,1,0:T(8,128)S(1)}, f32[16,8,96]{2,1,0:T(8,128)}, u32[]{:S(2)}) copy-start(f32[16,8,96]{2,1,0:T(8,128)} %price_ref.3) | copy-start | bytes 147460
  16.7 42.1 %copy-start.10 = (f32[8,96]{1,0:T(8,128)S(1)}, f32[8,96]{1,0:T(8,128)}, u32[]{:S(2)}) copy-start(f32[8,96]{1,0:T(8,128)} %limit_ref.1) | copy-start | bytes 9220
  16.7 42.1 %copy-start.14 = (s32[2,16]{1,0:T(2,128)S(1)}, s32[2,16]{1,0:T(2,128)}, u32[]{:S(2)}) copy-start(s32[2,16]{1,0:T(2,128)} %tree_ref.3) | copy-start | bytes 388

commit v2 on v1

v2 whole, which is shorter than its diff:
```python
import functools

import jax
import jax.numpy as jnp
from jax import lax
from jax.experimental import pallas as pl
from jax.experimental.pallas import tpu as pltpu
from jax.sharding import PartitionSpec as P

FEED = 128
PROX = 12
COARSE = 8
LANES = 128
MESH = pl.DeviceIdType.MESH
BF16 = jnp.bfloat16
F32 = jnp.float32


def round_up(value, unit):
    return (value + unit - 1) // unit * unit


def split3(value):
    first = value.astype(BF16)
    rest = value - first.astype(F32)
    second = rest.astype(BF16)
    third = (rest - second.astype(F32)).astype(BF16)
    return first, second, third


def solve_kernel(
    nodes, scen_size, bldg_size,
    demand_hbm, mult_hbm, prev_hbm, inv_hbm, tariff_hbm, price_hbm, limit_hbm, feeder_hbm, weight_hbm, tree_hbm,
    mine_ref, back_ref, full_ref, total_ref,
    demand, mult, prev, inv, tariff, price, limit, feeder, weight, tree,
    send, landed, keep, table, table_landed, hot, factor, cap, w_ref, fixed_ref, z_ref, u_ref, both_ref,
    packed, sums, sums_landed, theirs, load, load_first, load_mine, load_landed,
    in_sem, inv_sem, small_sem, send_sem, recv_sem, table_send, table_recv,
    rs_send, rs_recv, ag_send, ag_recv, on_send, on_recv,
    plan_send, plan_recv, pair_send, pair_recv, load_send, load_recv,
):
    scen, slots, count = demand.shape
    half = count // 2
    wide = 2 * scen
    groups, group_rows = sums.shape[:2]
    size = half // groups
    feeders = total_ref.shape[1]
    pieces = in_sem.shape[0]
    each = scen // pieces
    inv_pieces = inv_sem.shape[0]
    inv_each = slots // inv_pieces
    length = slots // 4
    chips = scen_size // 2
    chunk = group_rows // chips
    me, column = lax.axis_index("scen"), lax.axis_index("bldg")
    core = lax.rem(me, 2)
    chip = lax.div(me, 2)
    partner = (me + 1 - 2 * core, column)
    peers = [(lax.rem(me + 2 * k, scen_size), column) for k in range(1, chips)]
    beside = [(me, lax.rem(column + k, bldg_size)) for k in range(1, bldg_size)]
    own_lanes = pl.ds(pl.multiple_of(core * half, LANES), half)
    away_lanes = pl.ds(pl.multiple_of(half - core * half, LANES), half)

    def remote(src, dst, send, recv, device):
        copy = pltpu.make_async_remote_copy(
            src_ref=src, dst_ref=dst, send_sem=send, recv_sem=recv, device_id=device, device_id_type=MESH
        )
        copy.start()
        return copy

    def local(src, dst, sem):
        copy = pltpu.make_async_copy(src, dst, sem)
        copy.start()
        return copy

    barrier = pltpu.get_barrier_semaphore()
    for peer in [partner] + peers + beside:
        pl.semaphore_signal(barrier, inc=1, device_id=peer, device_id_type=MESH)
    small = [
        local(src, dst, small_sem.at[k])
        for k, (src, dst) in enumerate((
            (tariff_hbm, tariff), (price_hbm, price), (limit_hbm, limit),
            (feeder_hbm, feeder), (weight_hbm, weight), (tree_hbm, tree),
        ))
    ]
    loads = []
    for p in range(pieces):
        rows = pl.ds(p * each, each)
        loads.append([
            local(src.at[rows], dst.at[rows], in_sem.at[p, k])
            for k, (src, dst) in enumerate(((prev_hbm, prev), (demand_hbm, demand), (mult_hbm, mult)))
        ])
    inv_loads = []
    for p in range(inv_pieces):
        rows = pl.ds(p * inv_each, inv_each)
        inv_loads.append(local(inv_hbm.at[rows, :, own_lanes], inv.at[rows], inv_sem.at[p]))

    for copy in small:
        copy.wait()
    padded = table.shape[0]
    row = lax.broadcasted_iota(jnp.int32, (padded, scen), 0)
    hit = (row == 0) | (row == tree[0:1, :] + 1) | (row == tree[1:2, :] + (1 + COARSE))
    table[...] = jnp.where(hit, weight[...], 0.0)
    one = lax.broadcasted_iota(jnp.int32, (feeders, count), 0) == feeder[...]
    one = one.astype(F32).astype(BF16)
    for k in range(3):
        hot[k * feeders : (k + 1) * feeders, :] = one
    pl.semaphore_wait(barrier, chips + bldg_size - 1)
    table_copy = remote(table, table_landed, table_send, table_recv, partner)

    def fill(s, lanes, into):
        terms = jnp.concatenate(split3(price[s] + tariff[pl.ds(s, 1), :]), axis=0)
        paid = lax.dot_general(terms, hot[:, lanes], (((0,), (0,)), ((), ())), preferred_element_type=F32)
        before = prev[s, :, lanes]
        into[0, s] = 0.5 * before - (paid - demand[s, :, lanes]) - mult[s, :, lanes]
        into[1, s] = jnp.clip(before, 0.0, limit[:, lanes])

    swaps = []
    for p in range(pieces):
        for copy in loads[p]:
            copy.wait()
        for s in range(p * each, (p + 1) * each):
            fill(s, away_lanes, send)
        rows = pl.ds(p * each, each)
        swaps.append(remote(send.at[:, rows], landed.at[:, rows], send_sem.at[p], recv_sem.at[p], partner))
    for s in range(scen):
        fill(s, own_lanes, keep)

    def begin(k, source):
        fixed = jnp.transpose(source[0], (2, 0, 1))
        right = jnp.transpose(source[1], (2, 0, 1)) + fixed
        high = right.astype(BF16)
        fixed_ref[:, k * scen : (k + 1) * scen, :] = fixed
        both_ref[:, k * scen : (k + 1) * scen, :] = high
        both_ref[:, wide + k * scen : wide + (k + 1) * scen, :] = (right - high.astype(F32)).astype(BF16)

    begin(0, keep)
    cap[...] = jnp.transpose(limit[:, own_lanes], (1, 0))
    u_ref[...] = jnp.zeros_like(u_ref)
    for p in range(inv_pieces):
        inv_loads[p].wait()
        rows = slice(p * inv_each, (p + 1) * inv_each)
        exact = jnp.transpose(inv[rows], (2, 0, 1))
        high = exact.astype(BF16)
        w_ref[:, rows, :slots] = high
        w_ref[:, rows, LANES : LANES + slots] = (exact - high.astype(F32)).astype(BF16)
    table_copy.wait()
    lane = lax.broadcasted_iota(jnp.int32, (padded, LANES), 1)
    for s in range(scen):
        factor[s] = jnp.where(lane < size, table[:, s : s + 1], table_landed[:, s : s + 1])
    for copy in swaps:
        copy.wait_recv()
    begin(1, landed)

    def step(b):
        out = jnp.dot(both_ref[b], w_ref[b], preferred_element_type=F32)
        primal = out[:wide, :slots] + (out[:wide, LANES : LANES + slots] + out[wide:, :slots])
        moved = primal + u_ref[b]
        fresh = jnp.clip(moved, 0.0, cap[b : b + 1, :])
        dual = moved - fresh
        right = fresh - dual + fixed_ref[b]
        high = right.astype(BF16)
        z_ref[b] = fresh
        u_ref[b] = dual
        both_ref[b, :wide] = high
        both_ref[b, wide:] = (right - high.astype(F32)).astype(BF16)

    low_lanes = lax.broadcasted_iota(jnp.int32, (length, LANES), 1) < size
    tail = (nodes + 1) // 2 * length

    def add_up(g):
        part = slice(g * size, (g + 1) * size)
        packed[...] = jnp.concatenate(
            [
                jnp.transpose(z_ref[part, :scen, :], (1, 0, 2)),
                jnp.transpose(z_ref[part, scen:, :], (1, 0, 2)),
            ],
            axis=1,
        ).swapaxes(1, 2)[:, : 3 * length, :]
        whole = []
        for n in range(nodes):
            level = 0 if n == 0 else (1 if n <= COARSE else 2)
            acc = jnp.zeros((length, LANES), F32)
            for s in range(scen):
                acc = acc + factor[s, n : n + 1, :] * packed[s, level * length : (level + 1) * length, :]
            whole.append(acc + pltpu.roll(acc, size, 1))
            if n % 2 == 1 or n == nodes - 1:
                both = jnp.where(low_lanes, whole[n - n % 2], whole[n])
                sums[g, n // 2 * length : (n // 2 + 1) * length, :] = both
        rest = group_rows - tail
        counted = jnp.sum(table[...] + table_landed[...], axis=1, keepdims=True)
        sums[g, tail : tail + padded, :] = jnp.broadcast_to(counted, (padded, LANES))
        if rest > padded:
            sums[g, tail + padded :, :] = jnp.zeros((rest - padded, LANES), F32)

    def rows_of(index):
        return pl.ds(pl.multiple_of(index * chunk, 8), chunk)

    def scatter(g):
        return [
            remote(
                sums.at[g, rows_of(lax.div(peer[0], 2))], sums_landed.at[g, k],
                rs_send.at[g, k], rs_recv.at[g, k], peer,
            )
            for k, peer in enumerate(peers)
        ]

    def gather(g, scattered):
        for copy in scattered:
            copy.wait_recv()
        acc = sums[g, rows_of(chip), :]
        for k in range(chips - 1):
            acc = acc + sums_landed[g, k]
        full_ref[core, g, rows_of(chip), :] = acc
        spot = full_ref.at[core, g, rows_of(chip)]
        copies = [remote(spot, spot, ag_send.at[g, k], ag_recv.at[g, k], peer) for k, peer in enumerate(peers)]
        return copies, [remote(spot, spot, on_send.at[g, 0], on_recv.at[g, 0], partner)]

    def onward(g, gathered, passed):
        for k in range(1, chips):
            gathered[k - 1].wait_recv()
            spot = full_ref.at[core, g, rows_of(lax.rem(chip - k + chips, chips))]
            passed.append(remote(spot, spot, on_send.at[g, k], on_recv.at[g, k], partner))

    def solve(g, low, high):
        def twice(i, carry):
            for _ in range(2):
                for b in range(g * size, (g + 1) * size):
                    step(b)
            return carry

        lax.fori_loop(low, high, twice, 0)

    pending = []
    turns = PROX // 2
    done = []
    for g in range(groups):
        if g == 0:
            solve(g, 0, turns)
        else:
            solve(g, 0, turns // 3)
            gathered, passed = gather(g - 1, scattered)
            solve(g, turns // 3, 2 * turns // 3)
            onward(g - 1, gathered, passed)
            solve(g, 2 * turns // 3, turns)
            pending += scattered + gathered
            done += passed
        add_up(g)
        scattered = scatter(g)

    theirs[...] = jnp.transpose(z_ref[:, scen:, :], (1, 2, 0))
    plan_copy = remote(theirs, back_ref, plan_send, plan_recv, partner)
    mine_ref[...] = jnp.transpose(z_ref[:, :scen, :], (1, 2, 0))

    def loads_of(source):
        dims = (((1,), (1,)), ((), ()))
        one = hot[:feeders, own_lanes]
        for s in range(scen):
            value = source[s]
            high = value.astype(BF16)
            low = (value - high.astype(F32)).astype(BF16)
            yield s, lax.dot_general(one, high, dims, preferred_element_type=F32) + lax.dot_general(
                one, low, dims, preferred_element_type=F32
            )

    for s, value in loads_of(theirs):
        load[s] = value
    pair_load = remote(load, load_first, pair_send, pair_recv, partner)
    for s, value in loads_of(mine_ref):
        load_mine[s] = value
    last = groups - 1
    gathered, passed = gather(last, scattered)
    pair_load.wait_recv()
    load_mine[...] = load_mine[...] + load_first[...]
    spread_loads = [
        remote(load_mine, load_landed.at[k], load_send.at[k], load_recv.at[k], peer)
        for k, peer in enumerate(beside)
    ]
    onward(last, gathered, passed)
    total = load_mine[...]
    for k, copy in enumerate(spread_loads):
        copy.wait_recv()
        total = total + load_landed[k]
    total_ref[...] = total
    plan_copy.wait_recv()
    for copy in done + passed:
        copy.wait_recv()
    for copy in swaps + pending + scattered + gathered + done + passed + spread_loads + [plan_copy, pair_load]:
        copy.wait_send()


def solve(demand, mult, prev, inverse, tariff, price, limit, feeder, weights, tree, nodes, groups, rows):
    scen_size, bldg_size = lax.axis_size("scen"), lax.axis_size("bldg")
    chips = scen_size // 2
    scen, slots, count = demand.shape
    feeders = price.shape[1]
    half = count // 2
    length = slots // 4
    padded = round_up(nodes, 8)
    chunk = rows // chips
    vmem = pl.BlockSpec(memory_space=pltpu.VMEM)
    hbm = pl.BlockSpec(memory_space=pltpu.HBM)
    dma = pltpu.SemaphoreType.DMA
    big = pltpu.VMEM(demand.shape, F32)
    pair = pltpu.VMEM((2, scen, slots, half), F32)
    state = pltpu.VMEM((half, 2 * scen, slots), F32)
    held = lambda array: pltpu.VMEM(array.shape, array.dtype)
    loads = pltpu.VMEM((scen, feeders, slots), F32)
    return pl.pallas_call(
        functools.partial(solve_kernel, nodes, scen_size, bldg_size),
        in_specs=[hbm] * 10,
        out_specs=[vmem] * 4,
        out_shape=[
            jax.ShapeDtypeStruct((scen, slots, half), F32),
            jax.ShapeDtypeStruct((scen, slots, half), F32),
            jax.ShapeDtypeStruct((2, groups, rows, half), F32),
            jax.ShapeDtypeStruct((scen, feeders, slots), F32),
        ],
        scratch_shapes=[
            big, big, big,
            pltpu.VMEM((slots, slots, half), F32),
            held(tariff), held(price), held(limit), held(feeder), held(weights), held(tree),
            pair, pair, pair,
            pltpu.VMEM((padded, scen), F32), pltpu.VMEM((padded, scen), F32),
            pltpu.VMEM((3 * feeders, count), BF16),
            pltpu.VMEM((scen, padded, LANES), F32),
            pltpu.VMEM((half, slots), F32),
            pltpu.VMEM((half, slots, 2 * LANES), BF16),
            state, state, state,
            pltpu.VMEM((half, 4 * scen, slots), BF16),
            pltpu.VMEM((scen, 3 * length, LANES), F32),
            pltpu.VMEM((groups, rows, LANES), F32),
            pltpu.VMEM((groups, chips - 1, chunk, LANES), F32),
            pltpu.VMEM((scen, slots, half), F32),
            loads, loads, loads,
            pltpu.VMEM((bldg_size - 1, scen, feeders, slots), F32),
            dma((4, 3)), dma((slots // 16,)), dma((6,)), dma((4,)), dma((4,)), dma(()), dma(()),
            dma((groups, chips - 1)), dma((groups, chips - 1)),
            dma((groups, chips - 1)), dma((groups, chips - 1)),
            dma((groups, chips)), dma((groups, chips)),
            dma(()), dma(()), dma(()), dma(()),
            dma((bldg_size - 1,)), dma((bldg_size - 1,)),
        ],
        compiler_params=pltpu.CompilerParams(
            collective_id=0, has_side_effects=True, vmem_limit_bytes=42 * 2**20
        ),
        name="solve",
    )(*(pltpu.with_memory_space_constraint(x, pltpu.HBM) for x in (
        demand, mult, prev, inverse, tariff, price, limit, feeder, weights, tree)))


def spread_kernel(
    nodes, tree_ref, full_ref, mine_ref, back_ref, mult_ref, price_ref, load_ref, limit_ref,
    plan_ref, out_ref, new_price_ref, mean_ref,
):
    step = pl.program_id(0)
    each, slots, count = mult_ref.shape
    half = count // 2
    length = slots // 4
    tail = (nodes + 1) // 2 * length
    groups = full_ref.shape[1]
    size = half // groups
    core = lax.rem(lax.axis_index("scen"), 2)

    @pl.when(step == 0)
    def _():
        low_lanes = lax.broadcasted_iota(jnp.int32, (length, half), 1) < size
        for c in range(2):
            for n in range(nodes):
                count_row = full_ref[c, 0, tail + n : tail + n + 1, :]
                block = slice(n // 2 * length, (n // 2 + 1) * length)
                first = full_ref[c, 0, block, :]
                second = full_ref[c, 1, block, :]
                if n % 2 == 0:
                    share = jnp.where(low_lanes, first, pltpu.roll(second, size, 1))
                else:
                    share = jnp.where(low_lanes, pltpu.roll(first, size, 1), second)
                mean_ref[n, :, c * half : (c + 1) * half] = share / count_row

    for j in range(each):
        s = step * each + j
        places = (0, tree_ref[0, s] + 1, tree_ref[1, s] + (1 + COARSE))
        for source, offset in ((mine_ref, core * half), (back_ref, half - core * half)):
            lanes = pl.ds(pl.multiple_of(offset, LANES), half)
            plan_ref[j, :, lanes] = source[j]
            for level in range(4):
                part = slice(level * length, (level + 1) * length)
                plan = source[j, part, :]
                mean = plan if level == 3 else mean_ref[places[level], :, lanes]
                out_ref[j, part, lanes] = mult_ref[j, part, lanes] + 0.5 * (plan - mean)
    new_price_ref[...] = jnp.maximum(0.0, price_ref[...] + (load_ref[...] - limit_ref[...][None]) / FEED)


def spread(tree, full, mine, back, mult, price, load, limit, nodes):
    scen, slots, count = mult.shape
    feeders = price.shape[1]
    each = 4
    block = lambda *shape: pl.BlockSpec((each,) + shape, lambda i: (i, 0, 0))
    return pl.pallas_call(
        functools.partial(spread_kernel, nodes),
        grid=(scen // each,),
        in_specs=[
            pl.BlockSpec(memory_space=pltpu.SMEM),
            pl.BlockSpec(full.shape, lambda i: (0, 0, 0, 0)),
            block(slots, count // 2), block(slots, count // 2), block(slots, count),
            block(feeders, slots), block(feeders, slots),
            pl.BlockSpec(limit.shape, lambda i: (0, 0)),
        ],
        out_specs=[block(slots, count), block(slots, count), block(feeders, slots)],
        out_shape=[
            jax.ShapeDtypeStruct(mult.shape, F32),
            jax.ShapeDtypeStruct(mult.shape, F32),
            jax.ShapeDtypeStruct(price.shape, F32),
        ],
        scratch_shapes=[pltpu.VMEM((nodes, slots // 4, count), F32)],
        compiler_params=pltpu.CompilerParams(vmem_limit_bytes=24 * 2**20),
        name="spread",
    )(tree, full, mine, back, mult, price, load, limit)


def per_device(
    demand,
    tariff,
    feeder_price,
    multiplier,
    previous_mean,
    inverse,
    power_limit,
    weights,
    tree_node,
    building_feeder,
    feeder_limit,
):
    scen_size = lax.axis_size("scen")
    scen, count, slots = demand.shape
    nodes = 1 + COARSE + scen_size * scen // 8
    groups = 2
    rows = round_up((nodes + 1) // 2 * (slots // 4) + round_up(nodes, 8), 8 * (scen_size // 2))

    def turned(value):
        return jnp.transpose(value, (0, 2, 1))

    limit = jnp.transpose(power_limit, (1, 0))
    mult = turned(multiplier)
    mine, back, full, total = solve(
        turned(demand), mult, turned(previous_mean), jnp.transpose(inverse, (1, 2, 0)), tariff, feeder_price,
        limit, building_feeder.reshape(1, count), weights.reshape(1, scen), tree_node, nodes, groups, rows,
    )
    plan, new_multiplier, new_price = spread(
        tree_node, full, mine, back, mult, feeder_price, total, feeder_limit, nodes
    )
    return turned(plan), turned(new_multiplier), new_price


def solution(mesh):
    in_specs = (
        P("scen", "bldg", None),
        P("scen", None),
        P("scen", None, None),
        P("scen", "bldg", None),
        P("scen", "bldg", None),
        P("bldg", None, None),
        P("bldg", None),
        P("scen"),
        P(None, "scen"),
        P("bldg"),
        P(),
    )
    out_specs = (P("scen", "bldg", None), P("scen", "bldg", None), P("scen", None, None))
    return jax.shard_map(
        per_device, mesh=mesh, in_specs=in_specs, out_specs=out_specs, check_vma=False
    )
```

time: 62.2 us -> 47.5 us (0.76)
  local copies, waits for them, and re-layouts: 9.82 us -> 0.02 us
  Pallas kernels: 51.3 us -> 46.6 us
    unnamed x32 -> x8, local copies, waits for them, and re-layouts: 9.82 us -> 0.02 us
    pallas_call x3 -> x1, Pallas kernels: 48.2 us -> 43.6 us  [solve(): pl.pallas_call(functools.partial(solve_kernel, nodes, scen_size, bldg_siz...]
where the time goes in v2:
time: 47.5 us; the launch traced here: 47.4 us
  Pallas kernels  46.6 us (98%)
  between operations  0.71 us (1%)
    pallas_call x1, Pallas kernels, solve(): pl.pallas_call(functools.partial(solve_kernel, nodes, scen_size, bldg_siz...  43.6 us
    pallas_call x1, Pallas kernels, spread(): pl.pallas_call(functools.partial(spread_kernel, nodes), grid=(scen // eac...  3.02 us

profile of v2, /device:TPU:0, one launch (start us, length us, event | category | flops | bytes accessed | tf_op | source)
XLA Modules:
  0.0 47.4 jit_solution(2636652609383800970)
XLA Ops:
  0.6 0.0 copy-start
  0.6 0.0 copy-start.1
  0.7 0.0 copy-start.2
  0.7 0.0 copy-start.3
  0.7 43.6 %solve.1 = (f32[16,96,128]{2,1,0:T(8,128)S(1)}, f32[16,96,128]{2,1,0:T(8,128)S(1)}, f32[2,2,352,128]{3,2,1,0:T(8,128)S(1)}, f32[16,8,96]{2,1,0:T(8,128)S(1)}) custom-call(f32[16,96,256]{2,1,0:T(8,128)} %bitcast.12, f32[16,96,256]{2,1,0:T(8,128)} %bitcast.9, f32[16,96,256]{2,1,0:T(8,128)} %bitcast.13, f32[96,96,256]{2,1,0:T(8,128)} %bitcast.11, ...), custom_call_target="tpu_custom_call" | custom-call | tf_op jit(solution)/shard_map/solve/pallas_call | solution.py:309
  44.3 0.0 copy-done
  44.3 0.0 copy-done.1
  44.3 0.0 copy-done.2
  44.3 0.0 copy-done.3
  44.3 3.0 %spread.1 = (f32[16,96,256]{2,1,0:T(8,128)}, f32[16,96,256]{2,1,0:T(8,128)}, f32[16,8,96]{2,1,0:T(8,128)}) custom-call(s32[2,16]{1,0:T(2,128)S(1)} %copy-done.3, f32[2,2,352,128]{3,2,1,0:T(8,128)S(1)} %get-tuple-element.10.full_ref, f32[16,96,128]{2,1,0:T(8,128)S(1)} %get-tuple-element.11.mine_ref, f32[16,96,128]{2,1,0:T(8,128)S(1)} %get-tuple-element.12.back_ref, ...), custom_call_target="tpu_custom_call" | custom-call | tf_op jit(solution)/shard_map/spread/pallas_call | solution.py:399
Async XLA Ops:
  0.6 43.7 %copy-start = (f32[16,256,96]{1,2,0:T(8,128)S(1)}, f32[16,256,96]{1,2,0:T(8,128)}, u32[]{:S(2)}) copy-start(f32[16,256,96]{1,2,0:T(8,128)} %param.14) | copy-start | bytes 4718596
  0.6 43.7 %copy-start.1 = (f32[16,8,96]{2,1,0:T(8,128)S(1)}, f32[16,8,96]{2,1,0:T(8,128)}, u32[]{:S(2)}) copy-start(f32[16,8,96]{2,1,0:T(8,128)} %price_ref.1) | copy-start | bytes 147460
  0.7 43.7 %copy-start.2 = (f32[8,96]{1,0:T(8,128)S(1)}, f32[8,96]{1,0:T(8,128)}, u32[]{:S(2)}) copy-start(f32[8,96]{1,0:T(8,128)} %limit_ref.1) | copy-start | bytes 9220
  0.7 43.7 %copy-start.3 = (s32[2,16]{1,0:T(2,128)S(1)}, s32[2,16]{1,0:T(2,128)}, u32[]{:S(2)}) copy-start(s32[2,16]{1,0:T(2,128)} %tree_ref.1) | copy-start | bytes 388

commit v3 on v2

--- a/solution.py
+++ b/solution.py
@@ -34,7 +34,7 @@
     mine_ref, back_ref, full_ref, total_ref,
     demand, mult, prev, inv, tariff, price, limit, feeder, weight, tree,
     send, landed, keep, table, table_landed, hot, factor, cap, w_ref, fixed_ref, z_ref, u_ref, both_ref,
-    packed, sums, sums_landed, theirs, load, load_first, load_mine, load_landed,
+    packed, sums, sums_landed, theirs, load, load_other, load_sent, load_first, load_mine, load_landed,
     in_sem, inv_sem, small_sem, send_sem, recv_sem, table_send, table_recv,
     rs_send, rs_recv, ag_send, ag_recv, on_send, on_recv,
     plan_send, plan_recv, pair_send, pair_recv, load_send, load_recv,
@@ -44,7 +44,7 @@
     wide = 2 * scen
     groups, group_rows = sums.shape[:2]
     size = half // groups
-    feeders = total_ref.shape[1]
+    feeders = price.shape[1]
     pieces = in_sem.shape[0]
     each = scen // pieces
     inv_pieces = inv_sem.shape[0]
@@ -61,10 +61,13 @@
     own_lanes = pl.ds(pl.multiple_of(core * half, LANES), half)
     away_lanes = pl.ds(pl.multiple_of(half - core * half, LANES), half)
 
-    def remote(src, dst, send, recv, device):
-        copy = pltpu.make_async_remote_copy(
+    def described(src, dst, send, recv, device):
+        return pltpu.make_async_remote_copy(
             src_ref=src, dst_ref=dst, send_sem=send, recv_sem=recv, device_id=device, device_id_type=MESH
         )
+
+    def remote(*args):
+        copy = described(*args)
         copy.start()
         return copy
 
@@ -90,10 +93,9 @@
             local(src.at[rows], dst.at[rows], in_sem.at[p, k])
             for k, (src, dst) in enumerate(((prev_hbm, prev), (demand_hbm, demand), (mult_hbm, mult)))
         ])
-    inv_loads = []
     for p in range(inv_pieces):
         rows = pl.ds(p * inv_each, inv_each)
-        inv_loads.append(local(inv_hbm.at[rows, :, own_lanes], inv.at[rows], inv_sem.at[p]))
+        local(inv_hbm.at[rows, :, own_lanes], inv.at[rows], inv_sem.at[p])
 
     for copy in small:
         copy.wait()
@@ -137,13 +139,17 @@
     begin(0, keep)
     cap[...] = jnp.transpose(limit[:, own_lanes], (1, 0))
     u_ref[...] = jnp.zeros_like(u_ref)
-    for p in range(inv_pieces):
-        inv_loads[p].wait()
-        rows = slice(p * inv_each, (p + 1) * inv_each)
+
+    def turn(p, carry):
+        rows = pl.ds(pl.multiple_of(p * inv_each, inv_each), inv_each)
+        pltpu.make_async_copy(inv_hbm.at[rows, :, own_lanes], inv.at[rows], inv_sem.at[p]).wait()
         exact = jnp.transpose(inv[rows], (2, 0, 1))
         high = exact.astype(BF16)
         w_ref[:, rows, :slots] = high
         w_ref[:, rows, LANES : LANES + slots] = (exact - high.astype(F32)).astype(BF16)
+        return carry
+
+    lax.fori_loop(0, inv_pieces, turn, 0)
     table_copy.wait()
     lane = lax.broadcasted_iota(jnp.int32, (padded, LANES), 1)
     for s in range(scen):
@@ -170,19 +176,42 @@
 
     def add_up(g):
         part = slice(g * size, (g + 1) * size)
-        packed[...] = jnp.concatenate(
+        packed[g] = jnp.concatenate(
             [
                 jnp.transpose(z_ref[part, :scen, :], (1, 0, 2)),
                 jnp.transpose(z_ref[part, scen:, :], (1, 0, 2)),
             ],
             axis=1,
-        ).swapaxes(1, 2)[:, : 3 * length, :]
+        ).swapaxes(1, 2)
+        lanes = pl.ds(pl.multiple_of(core * half, LANES), half)
+        member = hot[:feeders, lanes].astype(F32)
+        other = pltpu.roll(member, size, 1)
+        lower = lax.broadcasted_iota(jnp.int32, (feeders, half), 1) < size
+        mine, theirs = (member, other) if g == 0 else (other, member)
+        pick = jnp.concatenate(
+            [jnp.where(lower, mine, 0.0), jnp.where(lower, 0.0, theirs)], axis=0
+        ).astype(BF16)
+        for s in range(scen):
+            value = packed[g, s]
+            high = value.astype(BF16)
+            terms = jnp.concatenate([high, (value - high.astype(F32)).astype(BF16)], axis=0)
+            out = lax.dot_general(pick, terms, (((1,), (1,)), ((), ())), preferred_element_type=F32)
+            out = out[:, :slots] + out[:, slots:]
+            for k, into in enumerate((load, load_other)):
+                rows = slice(s * feeders, (s + 1) * feeders)
+                part_out = out[k * feeders : (k + 1) * feeders]
+                into[rows, :] = part_out if g == 0 else into[rows, :] + part_out
+        if g == groups - 1:
+            load_sent[...] = jnp.transpose(load_other[...], (1, 0))
+            pair_load().start()
+
+    def add_nodes(g):
         whole = []
         for n in range(nodes):
             level = 0 if n == 0 else (1 if n <= COARSE else 2)
             acc = jnp.zeros((length, LANES), F32)
             for s in range(scen):
-                acc = acc + factor[s, n : n + 1, :] * packed[s, level * length : (level + 1) * length, :]
+                acc = acc + factor[s, n : n + 1, :] * packed[g, s, level * length : (level + 1) * length, :]
             whole.append(acc + pltpu.roll(acc, size, 1))
             if n % 2 == 1 or n == nodes - 1:
                 both = jnp.where(low_lanes, whole[n - n % 2], whole[n])
@@ -196,96 +225,96 @@
     def rows_of(index):
         return pl.ds(pl.multiple_of(index * chunk, 8), chunk)
 
+    def spot(g, k):
+        return full_ref.at[core, g, rows_of(lax.rem(chip - k + chips, chips))]
+
     def scatter(g):
         return [
-            remote(
+            described(
                 sums.at[g, rows_of(lax.div(peer[0], 2))], sums_landed.at[g, k],
                 rs_send.at[g, k], rs_recv.at[g, k], peer,
             )
             for k, peer in enumerate(peers)
         ]
 
-    def gather(g, scattered):
-        for copy in scattered:
+    def gather(g):
+        return [
+            described(spot(g, 0), spot(g, 0), ag_send.at[g, k], ag_recv.at[g, k], peer)
+            for k, peer in enumerate(peers)
+        ]
+
+    def onward(g, k):
+        return described(spot(g, k), spot(g, k), on_send.at[g, k], on_recv.at[g, k], partner)
+
+    def reduce_chunk(g):
+        for copy in scatter(g):
             copy.wait_recv()
         acc = sums[g, rows_of(chip), :]
         for k in range(chips - 1):
             acc = acc + sums_landed[g, k]
         full_ref[core, g, rows_of(chip), :] = acc
-        spot = full_ref.at[core, g, rows_of(chip)]
-        copies = [remote(spot, spot, ag_send.at[g, k], ag_recv.at[g, k], peer) for k, peer in enumerate(peers)]
-        return copies, [remote(spot, spot, on_send.at[g, 0], on_recv.at[g, 0], partner)]
-
-    def onward(g, gathered, passed):
-        for k in range(1, chips):
-            gathered[k - 1].wait_recv()
-            spot = full_ref.at[core, g, rows_of(lax.rem(chip - k + chips, chips))]
-            passed.append(remote(spot, spot, on_send.at[g, k], on_recv.at[g, k], partner))
-
-    def solve(g, low, high):
-        def twice(i, carry):
+        for copy in gather(g):
+            copy.start()
+        onward(g, 0).start()
+
+    def pass_on(g):
+        for k, copy in enumerate(gather(g)):
+            copy.wait_recv()
+            onward(g, k + 1).start()
+
+    def pair_load():
+        return described(load_sent, load_first, pair_send, pair_recv, partner)
+
+    turns = PROX // 2
+    for g in range(groups):
+
+        def twice(i, carry, g=g):
+            if g > 0:
+                pl.when(i == turns // 2)(functools.partial(reduce_chunk, g - 1))
+                pl.when(i == turns - 1)(functools.partial(pass_on, g - 1))
             for _ in range(2):
                 for b in range(g * size, (g + 1) * size):
                     step(b)
             return carry
 
-        lax.fori_loop(low, high, twice, 0)
-
-    pending = []
-    turns = PROX // 2
-    done = []
-    for g in range(groups):
-        if g == 0:
-            solve(g, 0, turns)
-        else:
-            solve(g, 0, turns // 3)
-            gathered, passed = gather(g - 1, scattered)
-            solve(g, turns // 3, 2 * turns // 3)
-            onward(g - 1, gathered, passed)
-            solve(g, 2 * turns // 3, turns)
-            pending += scattered + gathered
-            done += passed
+        lax.fori_loop(0, turns, twice, 0)
         add_up(g)
-        scattered = scatter(g)
-
-    theirs[...] = jnp.transpose(z_ref[:, scen:, :], (1, 2, 0))
-    plan_copy = remote(theirs, back_ref, plan_send, plan_recv, partner)
-    mine_ref[...] = jnp.transpose(z_ref[:, :scen, :], (1, 2, 0))
-
-    def loads_of(source):
-        dims = (((1,), (1,)), ((), ()))
-        one = hot[:feeders, own_lanes]
-        for s in range(scen):
-            value = source[s]
-            high = value.astype(BF16)
-            low = (value - high.astype(F32)).astype(BF16)
-            yield s, lax.dot_general(one, high, dims, preferred_element_type=F32) + lax.dot_general(
-                one, low, dims, preferred_element_type=F32
-            )
-
-    for s, value in loads_of(theirs):
-        load[s] = value
-    pair_load = remote(load, load_first, pair_send, pair_recv, partner)
-    for s, value in loads_of(mine_ref):
-        load_mine[s] = value
-    last = groups - 1
-    gathered, passed = gather(last, scattered)
-    pair_load.wait_recv()
-    load_mine[...] = load_mine[...] + load_first[...]
-    spread_loads = [
+        add_nodes(g)
+        for copy in scatter(g):
+            copy.start()
+
+    pair_load().wait_recv()
+    load_mine[...] = jnp.transpose(load[...], (1, 0)) + load_first[...]
+    load_copies = [
         remote(load_mine, load_landed.at[k], load_send.at[k], load_recv.at[k], peer)
         for k, peer in enumerate(beside)
     ]
-    onward(last, gathered, passed)
+    low_half = lax.broadcasted_iota(jnp.int32, (slots, LANES), 1) < size
+
+    def unpack(s, carry):
+        first, second = packed[0, s], packed[1, s]
+        theirs[s] = jnp.where(low_half, pltpu.roll(first, size, 1), second)
+        mine_ref[s] = jnp.where(low_half, first, pltpu.roll(second, size, 1))
+        return carry
+
+    lax.fori_loop(0, scen, unpack, 0)
+    plan_copy = remote(theirs, back_ref, plan_send, plan_recv, partner)
+    last = groups - 1
+    reduce_chunk(last)
+    pass_on(last)
     total = load_mine[...]
-    for k, copy in enumerate(spread_loads):
+    for k, copy in enumerate(load_copies):
         copy.wait_recv()
         total = total + load_landed[k]
-    total_ref[...] = total
+    total_ref[...] = jnp.transpose(total, (1, 0))
     plan_copy.wait_recv()
-    for copy in done + passed:
-        copy.wait_recv()
-    for copy in swaps + pending + scattered + gathered + done + passed + spread_loads + [plan_copy, pair_load]:
+    sent = swaps + load_copies + [plan_copy, pair_load()]
+    for g in range(groups):
+        passed = [onward(g, k) for k in range(chips)]
+        for copy in passed:
+            copy.wait_recv()
+        sent = sent + scatter(g) + gather(g) + passed
+    for copy in sent:
         copy.wait_send()
 
 
@@ -305,7 +334,8 @@
     pair = pltpu.VMEM((2, scen, slots, half), F32)
     state = pltpu.VMEM((half, 2 * scen, slots), F32)
     held = lambda array: pltpu.VMEM(array.shape, array.dtype)
-    loads = pltpu.VMEM((scen, feeders, slots), F32)
+    flat = pltpu.VMEM((scen * feeders, slots), F32)
+    loads = pltpu.VMEM((slots, scen * feeders), F32)
     return pl.pallas_call(
         functools.partial(solve_kernel, nodes, scen_size, bldg_size),
         in_specs=[hbm] * 10,
@@ -314,7 +344,7 @@
             jax.ShapeDtypeStruct((scen, slots, half), F32),
             jax.ShapeDtypeStruct((scen, slots, half), F32),
             jax.ShapeDtypeStruct((2, groups, rows, half), F32),
-            jax.ShapeDtypeStruct((scen, feeders, slots), F32),
+            jax.ShapeDtypeStruct((scen * feeders, slots), F32),
         ],
         scratch_shapes=[
             big, big, big,
@@ -328,12 +358,12 @@
             pltpu.VMEM((half, slots, 2 * LANES), BF16),
             state, state, state,
             pltpu.VMEM((half, 4 * scen, slots), BF16),
-            pltpu.VMEM((scen, 3 * length, LANES), F32),
+            pltpu.VMEM((groups, scen, slots, LANES), F32),
             pltpu.VMEM((groups, rows, LANES), F32),
             pltpu.VMEM((groups, chips - 1, chunk, LANES), F32),
             pltpu.VMEM((scen, slots, half), F32),
-            loads, loads, loads,
-            pltpu.VMEM((bldg_size - 1, scen, feeders, slots), F32),
+            flat, flat, loads, loads, loads,
+            pltpu.VMEM((bldg_size - 1, slots, scen * feeders), F32),
             dma((4, 3)), dma((slots // 16,)), dma((6,)), dma((4,)), dma((4,)), dma(()), dma(()),
             dma((groups, chips - 1)), dma((groups, chips - 1)),
             dma((groups, chips - 1)), dma((groups, chips - 1)),
@@ -447,7 +477,7 @@
         limit, building_feeder.reshape(1, count), weights.reshape(1, scen), tree_node, nodes, groups, rows,
     )
     plan, new_multiplier, new_price = spread(
-        tree_node, full, mine, back, mult, feeder_price, total, feeder_limit, nodes
+        tree_node, full, mine, back, mult, feeder_price, total.reshape(feeder_price.shape), feeder_limit, nodes
     )
     return turned(plan), turned(new_multiplier), new_price
 

time: 47.5 us -> 45.1 us (0.949)
  Pallas kernels: 46.6 us -> 44.3 us
    pallas_call x1, Pallas kernels: 43.6 us -> 41.2 us  [solve(): pl.pallas_call(functools.partial(solve_kernel, nodes, scen_size, bldg_siz...]
where the time goes in v3:
time: 45.1 us; the launch traced here: 45 us
  Pallas kernels  44.3 us (98%)
  between operations  0.71 us (2%)
    pallas_call x1, Pallas kernels, solve(): pl.pallas_call(functools.partial(solve_kernel, nodes, scen_size, bldg_siz...  41.2 us
    pallas_call x1, Pallas kernels, spread(): pl.pallas_call(functools.partial(spread_kernel, nodes), grid=(scen // eac...  3.02 us

profile of v3, /device:TPU:0, one launch (start us, length us, event | category | flops | bytes accessed | tf_op | source)
XLA Modules:
  0.0 45.0 jit_solution(3363476570806557407)
XLA Ops:
  0.6 0.0 copy-start
  0.6 0.0 copy-start.1
  0.7 0.0 copy-start.2
  0.7 0.0 copy-start.3
  0.7 41.2 %solve.1 = (f32[16,96,128]{2,1,0:T(8,128)S(1)}, f32[16,96,128]{2,1,0:T(8,128)S(1)}, f32[2,2,352,128]{3,2,1,0:T(8,128)S(1)}, f32[128,96]{1,0:T(8,128)S(1)}) custom-call(f32[16,96,256]{2,1,0:T(8,128)} %bitcast.14, f32[16,96,256]{2,1,0:T(8,128)} %bitcast.10, f32[16,96,256]{2,1,0:T(8,128)} %bitcast.15, f32[96,96,256]{2,1,0:T(8,128)} %bitcast.13, ...), custom_call_target="tpu_custom_call" | custom-call | tf_op jit(solution)/shard_map/solve/pallas_call | solution.py:339
  41.9 0.0 copy-done
  41.9 0.0 copy-done.1
  41.9 0.0 copy-done.2
  41.9 0.0 copy-done.3
  42.0 3.0 %spread.1 = (f32[16,96,256]{2,1,0:T(8,128)}, f32[16,96,256]{2,1,0:T(8,128)}, f32[16,8,96]{2,1,0:T(8,128)}) custom-call(s32[2,16]{1,0:T(2,128)S(1)} %copy-done.3, f32[2,2,352,128]{3,2,1,0:T(8,128)S(1)} %get-tuple-element.10.full_ref, f32[16,96,128]{2,1,0:T(8,128)S(1)} %get-tuple-element.11.mine_ref, f32[16,96,128]{2,1,0:T(8,128)S(1)} %get-tuple-element.12.back_ref, ...), custom_call_target="tpu_custom_call" | custom-call | tf_op jit(solution)/shard_map/spread/pallas_call | solution.py:429
Async XLA Ops:
  0.6 41.3 %copy-start = (f32[16,256,96]{1,2,0:T(8,128)S(1)}, f32[16,256,96]{1,2,0:T(8,128)}, u32[]{:S(2)}) copy-start(f32[16,256,96]{1,2,0:T(8,128)} %param.14) | copy-start | bytes 4718596
  0.6 41.3 %copy-start.1 = (f32[16,8,96]{2,1,0:T(8,128)S(1)}, f32[16,8,96]{2,1,0:T(8,128)}, u32[]{:S(2)}) copy-start(f32[16,8,96]{2,1,0:T(8,128)} %price_ref.1) | copy-start | bytes 147460
  0.7 41.3 %copy-start.2 = (f32[8,96]{1,0:T(8,128)S(1)}, f32[8,96]{1,0:T(8,128)}, u32[]{:S(2)}) copy-start(f32[8,96]{1,0:T(8,128)} %limit_ref.1) | copy-start | bytes 9220
  0.7 41.3 %copy-start.3 = (s32[2,16]{1,0:T(2,128)S(1)}, s32[2,16]{1,0:T(2,128)}, u32[]{:S(2)}) copy-start(s32[2,16]{1,0:T(2,128)} %tree_ref.1) | copy-start | bytes 388

commit v4 on v3

--- a/solution.py
+++ b/solution.py
@@ -42,7 +42,7 @@
     scen, slots, count = demand.shape
     half = count // 2
     wide = 2 * scen
-    groups, group_rows = sums.shape[:2]
+    groups = sums.shape[0]
     size = half // groups
     feeders = price.shape[1]
     pieces = in_sem.shape[0]
@@ -51,7 +51,9 @@
     inv_each = slots // inv_pieces
     length = slots // 4
     chips = scen_size // 2
-    chunk = group_rows // chips
+    pairs = (nodes + 1) // 2
+    unit = 8 * chips
+    group_rows = [sums.shape[1]] + [round_up(pairs * length, unit)] * (groups - 1)
     me, column = lax.axis_index("scen"), lax.axis_index("bldg")
     core = lax.rem(me, 2)
     chip = lax.div(me, 2)
@@ -176,34 +178,24 @@
 
     def add_up(g):
         part = slice(g * size, (g + 1) * size)
-        packed[g] = jnp.concatenate(
-            [
-                jnp.transpose(z_ref[part, :scen, :], (1, 0, 2)),
-                jnp.transpose(z_ref[part, scen:, :], (1, 0, 2)),
-            ],
-            axis=1,
-        ).swapaxes(1, 2)
+        turned = [jnp.transpose(z_ref[part, k * scen : (k + 1) * scen, :], (1, 0, 2)) for k in range(2)]
         lanes = pl.ds(pl.multiple_of(core * half, LANES), half)
         member = hot[:feeders, lanes].astype(F32)
-        other = pltpu.roll(member, size, 1)
-        lower = lax.broadcasted_iota(jnp.int32, (feeders, half), 1) < size
-        mine, theirs = (member, other) if g == 0 else (other, member)
-        pick = jnp.concatenate(
-            [jnp.where(lower, mine, 0.0), jnp.where(lower, 0.0, theirs)], axis=0
-        ).astype(BF16)
-        for s in range(scen):
-            value = packed[g, s]
-            high = value.astype(BF16)
-            terms = jnp.concatenate([high, (value - high.astype(F32)).astype(BF16)], axis=0)
-            out = lax.dot_general(pick, terms, (((1,), (1,)), ((), ())), preferred_element_type=F32)
-            out = out[:, :slots] + out[:, slots:]
-            for k, into in enumerate((load, load_other)):
+        pick = (member if g == 0 else pltpu.roll(member, size, 1))[:, :size].astype(BF16)
+        for k, into in ((1, load_other), (0, load)):
+            for s in range(scen):
+                value = turned[k][s]
+                high = value.astype(BF16)
+                low = (value - high.astype(F32)).astype(BF16)
+                out = jnp.dot(pick, high, preferred_element_type=F32) + jnp.dot(
+                    pick, low, preferred_element_type=F32
+                )
                 rows = slice(s * feeders, (s + 1) * feeders)
-                part_out = out[k * feeders : (k + 1) * feeders]
-                into[rows, :] = part_out if g == 0 else into[rows, :] + part_out
+                into[rows, :] = out if g == 0 else into[rows, :] + out
         if g == groups - 1:
             load_sent[...] = jnp.transpose(load_other[...], (1, 0))
             pair_load().start()
+        packed[g] = jnp.concatenate(turned, axis=1).swapaxes(1, 2)
 
     def add_nodes(g):
         whole = []
@@ -216,22 +208,27 @@
             if n % 2 == 1 or n == nodes - 1:
                 both = jnp.where(low_lanes, whole[n - n % 2], whole[n])
                 sums[g, n // 2 * length : (n // 2 + 1) * length, :] = both
-        rest = group_rows - tail
+        rest = group_rows[g] - tail
+        if g > 0:
+            if rest > 0:
+                sums[g, tail : tail + rest, :] = jnp.zeros((rest, LANES), F32)
+            return
         counted = jnp.sum(table[...] + table_landed[...], axis=1, keepdims=True)
         sums[g, tail : tail + padded, :] = jnp.broadcast_to(counted, (padded, LANES))
         if rest > padded:
-            sums[g, tail + padded :, :] = jnp.zeros((rest - padded, LANES), F32)
-
-    def rows_of(index):
+            sums[g, tail + padded : tail + rest, :] = jnp.zeros((rest - padded, LANES), F32)
+
+    def rows_of(g, index):
+        chunk = group_rows[g] // chips
         return pl.ds(pl.multiple_of(index * chunk, 8), chunk)
 
     def spot(g, k):
-        return full_ref.at[core, g, rows_of(lax.rem(chip - k + chips, chips))]
+        return full_ref.at[core, g, rows_of(g, lax.rem(chip - k + chips, chips))]
 
     def scatter(g):
         return [
             described(
-                sums.at[g, rows_of(lax.div(peer[0], 2))], sums_landed.at[g, k],
+                sums.at[g, rows_of(g, lax.div(peer[0], 2))], sums_landed.at[g, k, pl.ds(0, group_rows[g] // chips)],
                 rs_send.at[g, k], rs_recv.at[g, k], peer,
             )
             for k, peer in enumerate(peers)
@@ -249,10 +246,10 @@
     def reduce_chunk(g):
         for copy in scatter(g):
             copy.wait_recv()
-        acc = sums[g, rows_of(chip), :]
+        acc = sums[g, rows_of(g, chip), :]
         for k in range(chips - 1):
-            acc = acc + sums_landed[g, k]
-        full_ref[core, g, rows_of(chip), :] = acc
+            acc = acc + sums_landed[g, k, : group_rows[g] // chips]
+        full_ref[core, g, rows_of(g, chip), :] = acc
         for copy in gather(g):
             copy.start()
         onward(g, 0).start()
@@ -381,68 +378,84 @@
 
 def spread_kernel(
     nodes, tree_ref, full_ref, mine_ref, back_ref, mult_ref, price_ref, load_ref, limit_ref,
-    plan_ref, out_ref, new_price_ref, mean_ref,
+    plan_hbm, out_hbm, new_price_hbm, mean_ref, out_ref, new_price, plan_sem, out_sem, price_sem,
 ):
-    step = pl.program_id(0)
-    each, slots, count = mult_ref.shape
+    scen, slots, count = mult_ref.shape
     half = count // 2
     length = slots // 4
     tail = (nodes + 1) // 2 * length
     groups = full_ref.shape[1]
     size = half // groups
+    pieces = out_sem.shape[0]
+    each = scen // pieces
     core = lax.rem(lax.axis_index("scen"), 2)
-
-    @pl.when(step == 0)
-    def _():
-        low_lanes = lax.broadcasted_iota(jnp.int32, (length, half), 1) < size
-        for c in range(2):
-            for n in range(nodes):
-                count_row = full_ref[c, 0, tail + n : tail + n + 1, :]
-                block = slice(n // 2 * length, (n // 2 + 1) * length)
-                first = full_ref[c, 0, block, :]
-                second = full_ref[c, 1, block, :]
-                if n % 2 == 0:
-                    share = jnp.where(low_lanes, first, pltpu.roll(second, size, 1))
-                else:
-                    share = jnp.where(low_lanes, pltpu.roll(first, size, 1), second)
-                mean_ref[n, :, c * half : (c + 1) * half] = share / count_row
-
-    for j in range(each):
-        s = step * each + j
+    sides = [
+        (source, pl.ds(pl.multiple_of(offset, LANES), half))
+        for source, offset in ((mine_ref, core * half), (back_ref, half - core * half))
+    ]
+    copies = []
+    for p in range(pieces):
+        rows = pl.ds(p * each, each)
+        for k, (source, lanes) in enumerate(sides):
+            copies.append(pltpu.make_async_copy(source.at[rows], plan_hbm.at[rows, :, lanes], plan_sem.at[p, k]))
+            copies[-1].start()
+    new_price[...] = jnp.maximum(0.0, price_ref[...] + (load_ref[...] - limit_ref[...][None]) / FEED)
+    copies.append(pltpu.make_async_copy(new_price, new_price_hbm, price_sem))
+    copies[-1].start()
+
+    low_lanes = lax.broadcasted_iota(jnp.int32, (length, half), 1) < size
+    for c in range(2):
+        for n in range(nodes):
+            count_row = full_ref[c, 0, tail + n : tail + n + 1, :]
+            block = slice(n // 2 * length, (n // 2 + 1) * length)
+            first = full_ref[c, 0, block, :]
+            second = full_ref[c, 1, block, :]
+            if n % 2 == 0:
+                share = jnp.where(low_lanes, first, pltpu.roll(second, size, 1))
+            else:
+                share = jnp.where(low_lanes, pltpu.roll(first, size, 1), second)
+            mean_ref[n, :, c * half : (c + 1) * half] = share / count_row
+
+    def finish(s, carry):
         places = (0, tree_ref[0, s] + 1, tree_ref[1, s] + (1 + COARSE))
-        for source, offset in ((mine_ref, core * half), (back_ref, half - core * half)):
-            lanes = pl.ds(pl.multiple_of(offset, LANES), half)
-            plan_ref[j, :, lanes] = source[j]
+        for source, lanes in sides:
             for level in range(4):
                 part = slice(level * length, (level + 1) * length)
-                plan = source[j, part, :]
+                plan = source[s, part, :]
                 mean = plan if level == 3 else mean_ref[places[level], :, lanes]
-                out_ref[j, part, lanes] = mult_ref[j, part, lanes] + 0.5 * (plan - mean)
-    new_price_ref[...] = jnp.maximum(0.0, price_ref[...] + (load_ref[...] - limit_ref[...][None]) / FEED)
+                out_ref[s, part, lanes] = mult_ref[s, part, lanes] + 0.5 * (plan - mean)
+        return carry
+
+    for p in range(pieces):
+        lax.fori_loop(p * each, (p + 1) * each, finish, 0)
+        rows = pl.ds(p * each, each)
+        copies.append(pltpu.make_async_copy(out_ref.at[rows], out_hbm.at[rows], out_sem.at[p]))
+        copies[-1].start()
+    for copy in copies:
+        copy.wait()
 
 
 def spread(tree, full, mine, back, mult, price, load, limit, nodes):
     scen, slots, count = mult.shape
-    feeders = price.shape[1]
-    each = 4
-    block = lambda *shape: pl.BlockSpec((each,) + shape, lambda i: (i, 0, 0))
+    pieces = 4
+    vmem = pl.BlockSpec(memory_space=pltpu.VMEM)
+    hbm = pl.BlockSpec(memory_space=pltpu.HBM)
+    dma = pltpu.SemaphoreType.DMA
     return pl.pallas_call(
         functools.partial(spread_kernel, nodes),
-        grid=(scen // each,),
-        in_specs=[
-            pl.BlockSpec(memory_space=pltpu.SMEM),
-            pl.BlockSpec(full.shape, lambda i: (0, 0, 0, 0)),
-            block(slots, count // 2), block(slots, count // 2), block(slots, count),
-            block(feeders, slots), block(feeders, slots),
-            pl.BlockSpec(limit.shape, lambda i: (0, 0)),
-        ],
-        out_specs=[block(slots, count), block(slots, count), block(feeders, slots)],
+        in_specs=[pl.BlockSpec(memory_space=pltpu.SMEM)] + [vmem] * 7,
+        out_specs=[hbm] * 3,
         out_shape=[
             jax.ShapeDtypeStruct(mult.shape, F32),
             jax.ShapeDtypeStruct(mult.shape, F32),
             jax.ShapeDtypeStruct(price.shape, F32),
         ],
-        scratch_shapes=[pltpu.VMEM((nodes, slots // 4, count), F32)],
+        scratch_shapes=[
+            pltpu.VMEM((nodes, slots // 4, count), F32),
+            pltpu.VMEM(mult.shape, F32),
+            pltpu.VMEM(price.shape, F32),
+            dma((pieces, 2)), dma((pieces,)), dma(()),
+        ],
         compiler_params=pltpu.CompilerParams(vmem_limit_bytes=24 * 2**20),
         name="spread",
     )(tree, full, mine, back, mult, price, load, limit)

time: 45.1 us -> 43.9 us (0.973)
  Pallas kernels: 44.3 us -> 43 us
    pallas_call x1, Pallas kernels: 3.02 us -> 2.35 us  [spread(): pl.pallas_call(functools.partial(spread_kernel, nodes), in_specs=[pl.Bloc...]
    pallas_call x1, Pallas kernels: 41.2 us -> 40.6 us  [solve(): pl.pallas_call(functools.partial(solve_kernel, nodes, scen_size, bldg_siz...]
where the time goes in v4:
time: 43.9 us; the launch traced here: 43.7 us
  Pallas kernels  43 us (98%)
  between operations  0.71 us (2%)
    pallas_call x1, Pallas kernels, solve(): pl.pallas_call(functools.partial(solve_kernel, nodes, scen_size, bldg_siz...  40.6 us
    pallas_call x1, Pallas kernels, spread(): pl.pallas_call(functools.partial(spread_kernel, nodes), in_specs=[pl.Bloc...  2.35 us

profile of v4, /device:TPU:0, one launch (start us, length us, event | category | flops | bytes accessed | tf_op | source)
XLA Modules:
  0.0 43.7 jit_solution(15943879474239560638)
XLA Ops:
  0.6 0.0 copy-start
  0.6 0.0 copy-start.1
  0.7 0.0 copy-start.2
  0.7 0.0 copy-start.3
  0.7 40.6 %solve.1 = (f32[16,96,128]{2,1,0:T(8,128)S(1)}, f32[16,96,128]{2,1,0:T(8,128)S(1)}, f32[2,2,352,128]{3,2,1,0:T(8,128)S(1)}, f32[128,96]{1,0:T(8,128)S(1)}) custom-call(f32[16,96,256]{2,1,0:T(8,128)} %bitcast.14, f32[16,96,256]{2,1,0:T(8,128)} %bitcast.10, f32[16,96,256]{2,1,0:T(8,128)} %bitcast.15, f32[96,96,256]{2,1,0:T(8,128)} %bitcast.13, ...), custom_call_target="tpu_custom_call" | custom-call | tf_op jit(solution)/shard_map/solve/pallas_call | solution.py:336
  41.3 0.0 copy-done
  41.3 0.0 copy-done.1
  41.3 0.0 copy-done.2
  41.3 0.0 copy-done.3
  41.4 2.3 %spread.1 = (f32[16,96,256]{2,1,0:T(8,128)}, f32[16,96,256]{2,1,0:T(8,128)}, f32[16,8,96]{2,1,0:T(8,128)}) custom-call(s32[2,16]{1,0:T(2,128)S(1)} %copy-done.3, f32[2,2,352,128]{3,2,1,0:T(8,128)S(1)} %get-tuple-element.10.full_ref, f32[16,96,128]{2,1,0:T(8,128)S(1)} %get-tuple-element.11.mine_ref, f32[16,96,128]{2,1,0:T(8,128)S(1)} %get-tuple-element.12.back_ref, ...), custom_call_target="tpu_custom_call" | custom-call | tf_op jit(solution)/shard_map/spread/pallas_call | solution.py:444
Async XLA Ops:
  0.6 40.7 %copy-start = (f32[16,256,96]{1,2,0:T(8,128)S(1)}, f32[16,256,96]{1,2,0:T(8,128)}, u32[]{:S(2)}) copy-start(f32[16,256,96]{1,2,0:T(8,128)} %param.14) | copy-start | bytes 4718596
  0.6 40.7 %copy-start.1 = (f32[16,8,96]{2,1,0:T(8,128)S(1)}, f32[16,8,96]{2,1,0:T(8,128)}, u32[]{:S(2)}) copy-start(f32[16,8,96]{2,1,0:T(8,128)} %price_ref.1) | copy-start | bytes 147460
  0.7 40.7 %copy-start.2 = (f32[8,96]{1,0:T(8,128)S(1)}, f32[8,96]{1,0:T(8,128)}, u32[]{:S(2)}) copy-start(f32[8,96]{1,0:T(8,128)} %limit_ref.1) | copy-start | bytes 9220
  0.7 40.7 %copy-start.3 = (s32[2,16]{1,0:T(2,128)S(1)}, s32[2,16]{1,0:T(2,128)}, u32[]{:S(2)}) copy-start(s32[2,16]{1,0:T(2,128)} %tree_ref.1) | copy-start | bytes 388
